TPU v7x, 128 devices: a whole 4x4x4 slice. The times are simulated.
128 devices in a mesh: wide: 32 (over z, y, core), narrow: 4 (over x).
Axes of the slice: x: 4, y: 4, z: 4, core: 2. Of those that a mesh axis runs over, the one named last changes fastest.
Arguments:
- tokens: bfloat16 [16384, 2048], P(('wide', 'narrow')), may hold values from -6 to 6
- expert_ids: int32 [16384, 10], P(('wide', 'narrow')), may hold values from 0 to 255, all different within a row; in each aligned block of 128 rows (0 to 127, 128 to 255, ...) at most 7 rows name the same one
- combine: int32 [16384, 10], P(('wide', 'narrow')), may hold values from 8 to 63
- w_gate: bfloat16 [256, 2048, 512], P(('wide', 'narrow')), may hold values from -0.125 to 0.125
- w_up: bfloat16 [256, 2048, 512], P(('wide', 'narrow')), may hold values from -0.125 to 0.125
- w_down: bfloat16 [256, 512, 2048], P(('wide', 'narrow')), may hold values from -0.25 to 0.25
- shared_gate_up: bfloat16 [2, 2048, 512], P(None, None, 'narrow'), may hold values from -0.125 to 0.125
- shared_down: bfloat16 [512, 2048], P('narrow'), may hold values from -0.25 to 0.25
- gate_vector: bfloat16 [2048], replicated, may hold values from -0.25 to 0.25
Outputs:
- layer_out: bfloat16 [16384, 2048], P(('wide', 'narrow'))
Inputs may be any that keep to these rules, and one draw needn't show every extreme that they name: `expert_ids`: each row names 10 different experts. Among the 128 rows of one device no expert is named more than 7 times, and in every draw some device names some expert exactly 7 times. `combine`: an assignment's weight is its value divided by 256.
All inputs are finite; a program needn't handle non-finite values.
Results may differ from a plain program's by a relative error of at most 0.0054.
Values may be sent and summed in bfloat16 or wider, within the bound.
A program may use at most 128 MiB of HBM per device.

v0:
```python
import jax
import jax.numpy as jnp
from jax import lax
from jax.sharding import PartitionSpec as P

CAP = 7


def in_order(parts, dim):
    parts = jnp.moveaxis(parts, 0, dim)
    dims = parts.shape
    return parts.reshape(*dims[:dim], dims[dim] * dims[dim + 1], *dims[dim + 2 :])


def from_everyone(array, axis):
    devices = lax.axis_size(axis)
    return lax.all_to_all(
        jnp.broadcast_to(array[None], (devices, *array.shape)), axis, 0, 0, tiled=True
    )


def gathered_copies(array, axis, dim):
    return in_order(from_everyone(array, axis), dim)


def cut_along(array, dim, devices):
    before, after = (array.shape[:dim], array.shape[dim + 1 :])
    return jnp.moveaxis(array.reshape(*before, devices, -1, *after), dim, 0)


def sent_and_summed(array, axis, dim):
    devices = lax.axis_size(axis)
    parts = lax.all_to_all(cut_along(array, dim, devices), axis, 0, 0, tiled=True)
    return jnp.sum(parts, axis=0)


def slot_order(flat_ids, experts_total):
    columns = jnp.arange(experts_total, dtype=jnp.int32)
    onehot = (flat_ids[:, None] == columns[None, :]).astype(jnp.int32)
    before = jnp.cumsum(onehot, axis=0) - onehot
    return jnp.sum(before * onehot, axis=1)


def expert_block(received, w_gate, w_up, w_down):
    gate_part = jnp.einsum("secd,edf->secf", received, w_gate, preferred_element_type=jnp.float32)
    up_part = jnp.einsum("secd,edf->secf", received, w_up, preferred_element_type=jnp.float32)
    hidden = (jax.nn.silu(gate_part) * up_part).astype(jnp.bfloat16)
    return jnp.einsum("secf,efd->secd", hidden, w_down, preferred_element_type=jnp.float32).astype(
        jnp.bfloat16
    )


def on_device(
    tokens, expert_ids, combine, w_gate, w_up, w_down, shared_gate_up, shared_down, gate_vector
):
    tok_rows, model_width = tokens.shape
    top_count = expert_ids.shape[1]
    devices = lax.axis_size(("wide", "narrow"))
    local_experts = w_gate.shape[0]
    experts_total = local_experts * devices
    flat_ids = expert_ids.reshape(-1)
    positions = slot_order(flat_ids, experts_total)
    slot_index = flat_ids * CAP + positions
    repeated = jnp.repeat(tokens, top_count, axis=0)
    outgoing = (
        jnp.zeros((experts_total * CAP, model_width), jnp.bfloat16).at[slot_index].set(repeated)
    )
    outgoing = outgoing.reshape(devices, local_experts, CAP, model_width)
    produced = expert_block(
        lax.all_to_all(outgoing, ("wide", "narrow"), split_axis=0, concat_axis=0, tiled=True),
        w_gate,
        w_up,
        w_down,
    )
    returned = lax.all_to_all(produced, ("wide", "narrow"), split_axis=0, concat_axis=0, tiled=True)
    returned = returned.reshape(experts_total * CAP, model_width)
    returned_rows = returned[slot_index].reshape(tok_rows, top_count, model_width)
    mix_weights = combine.astype(jnp.float32) / 256.0
    routed = jnp.sum(returned_rows.astype(jnp.float32) * mix_weights[:, :, None], axis=1)
    shared_scale = jax.nn.sigmoid(jnp.dot(tokens, gate_vector, preferred_element_type=jnp.float32))
    gathered = gathered_copies(tokens, "narrow", 0)
    gate_up = jnp.einsum(
        "td,gdn->gtn", gathered, shared_gate_up, preferred_element_type=jnp.float32
    )
    shared_hidden = (jax.nn.silu(gate_up[0]) * gate_up[1]).astype(jnp.bfloat16)
    shared_out = sent_and_summed(
        jnp.dot(shared_hidden, shared_down, preferred_element_type=jnp.float32), "narrow", 0
    )
    layer_out = routed + shared_scale[:, None] * shared_out
    return layer_out.astype(jnp.bfloat16)


def solution(mesh):
    return jax.shard_map(
        on_device,
        mesh=mesh,
        in_specs=(
            P(("wide", "narrow"), None),
            P(("wide", "narrow"), None),
            P(("wide", "narrow"), None),
            P(("wide", "narrow"), None, None),
            P(("wide", "narrow"), None, None),
            P(("wide", "narrow"), None, None),
            P(None, None, "narrow"),
            P("narrow", None),
            P(),
        ),
        out_specs=P(("wide", "narrow"), None),
        check_vma=False,
    )
```

profile of v0, /device:TPU:1, one launch (start us, length us, event | category | flops | bytes accessed | tf_op | source)
XLA Modules:
  0.0 387.4 jit_solution(10730339333044288055)
XLA Ops:
  0.0 2.7 broadcast_in_dim.8
  2.7 4.8 %all-to-all-start.2 = ((bf16[4,128,2048]{2,1,0:T(8,128)(2,1)}), bf16[4,128,2048]{2,1,0:T(8,128)(2,1)}, u32[]{:S(2)}, u32[]{:S(2)}) async-start(bf16[4,128,2048]{2,1,0:T(8,128)(2,1)} %broadcast_in_dim.8), calls=%async_computation.2 | async-start | bytes 4194304 | tf_op jit(solution)/shard_map/all_to_all | solution.py:17
  7.6 0.1 eq.29
  8.0 0.3 fusion.13
  8.4 0.2 broadcast_add_fusion
  8.6 0.8 copy.44
  9.5 0.1 mul.53
  9.7 5.5 %broadcast_in_dim.7 = bf16[128,10,2048]{2,1,0:T(8,128)(2,1)} broadcast(bf16[128,2048]{1,0:T(8,128)(2,1)} %param.9), dimensions={0,2} | broadcast | bytes 5767168 | tf_op jit(solution)/shard_map/broadcast_in_dim | solution.py:64
  15.2 9.9 %reshape.86 = bf16[1280,2048]{1,0:T(8,128)(2,1)} reshape(bf16[128,10,2048]{2,1,0:T(8,128)(2,1)} %broadcast_in_dim.7) | data formatting | bytes 10485760 | tf_op jit(solution)/shard_map/reshape | solution.py:64
  25.1 0.5 fusion.25
  25.6 25.6 %scatter_custom_fusion = bf16[1792,2048]{1,0:T(8,128)(2,1)} fusion(s32[1280]{0:T(1024)S(1)} %fusion.34, bf16[1280,2048]{1,0:T(8,128)(2,1)} %reshape.86, bf16[]{:T(256)} %constant.7.clone.1), kind=kCustom, calls=%fused_computation.18 | custom fusion | bytes 7340544 | tf_op jit(solution)/shard_map/scatter | solution.py:66
  51.2 11.2 %reshape.70 = bf16[128,2,7,2048]{3,2,1,0:T(8,128)(2,1)} reshape(bf16[1792,2048]{1,0:T(8,128)(2,1)} %scatter_custom_fusion) | data formatting | bytes 14680064 | tf_op jit(solution)/shard_map/reshape | solution.py:68
  62.4 15.9 %copy.45 = bf16[128,2,7,2048]{3,1,2,0:T(2,128)(2,1)} copy(bf16[128,2,7,2048]{3,2,1,0:T(8,128)(2,1)} %reshape.70) | data formatting | bytes 14680064 | tf_op jit(solution)/shard_map/reshape | solution.py:68
  78.3 12.0 %all-to-all-start = ((bf16[128,2,7,2048]{3,1,2,0:T(2,128)(2,1)}), bf16[128,2,7,2048]{3,1,2,0:T(2,128)(2,1)}, u32[]{:S(2)}, u32[]{:S(2)}) async-start(bf16[128,2,7,2048]{3,1,2,0:T(2,128)(2,1)} %copy.45), calls=%async_computation | async-start | bytes 14680064 | tf_op jit(solution)/shard_map/all_to_all | solution.py:70
  90.3 2.4 convolution_bitcast_fusion
  93.0 2.7 fusion.31
  95.7 84.2 %all-to-all-done = bf16[128,2,7,2048]{3,1,2,0:T(2,128)(2,1)} async-done(((bf16[128,2,7,2048]{3,1,2,0:T(2,128)(2,1)}), bf16[128,2,7,2048]{3,1,2,0:T(2,128)(2,1)}, u32[]{:S(2)}, u32[]{:S(2)}) %all-to-all-start) | async-done | bytes 7340064 | tf_op jit(solution)/shard_map/all_to_all | solution.py:70
  179.9 4.9 %all-to-all-start.3 = ((f32[4,128,2048]{2,1,0:T(8,128)}), f32[4,128,2048]{2,1,0:T(8,128)}, u32[]{:S(2)}, u32[]{:S(2)}) async-start(f32[4,128,2048]{2,1,0:T(8,128)} %fusion.31), calls=%async_computation.3 | async-start | bytes 8388608 | tf_op jit(solution)/shard_map/all_to_all | solution.py:33
  184.7 10.4 %fusion.2 = f32[2,128,7,512]{3,1,2,0:T(8,128)} fusion(bf16[128,2,7,2048]{3,1,2,0:T(2,128)(2,1)} %all-to-all-done, bf16[2,2048,512]{2,1,0:T(8,128)(2,1)} %param.12), kind=kOutput, calls=%fused_computation.6 | convolution fusion | flops 3758096384 | bytes 15204352 | tf_op jit(solution)/shard_map/secd,edf->secf/dot_general | solution.py:45
  195.1 18.6 %convert_bitcast_fusion = bf16[128,2,7,2048]{3,0,2,1:T(8,128)(2,1)} fusion(bf16[2,512,2048]{2,1,0:T(8,128)(2,1)} %param.14, f32[2,128,7,512]{3,1,2,0:T(8,128)} %fusion.2, bf16[2,2048,512]{2,1,0:T(8,128)(2,1)} %param.13, bf16[128,2,7,2048]{3,1,2,0:T(2,128)(2,1)} %all-to-all-done), kind=kOutput, calls=%fused_computation.3 | convolution fusion | flops 7525367808 | bytes 26738688 | tf_op jit(solution)/shard_map/secf,efd->secd/dot_general | solution.py:48
  213.8 14.7 %copy.48 = bf16[128,2,7,2048]{3,1,2,0:T(2,128)(2,1)} copy(bf16[128,2,7,2048]{3,0,2,1:T(8,128)(2,1)} %convert_bitcast_fusion) | data formatting | bytes 14680064 | tf_op jit(solution)/shard_map/convert_element_type | solution.py:48
  228.4 5.1 %all-to-all-done.3 = f32[4,128,2048]{2,1,0:T(8,128)} async-done(((f32[4,128,2048]{2,1,0:T(8,128)}), f32[4,128,2048]{2,1,0:T(8,128)}, u32[]{:S(2)}, u32[]{:S(2)}) %all-to-all-start.3) | async-done | bytes 4194336 | tf_op jit(solution)/shard_map/all_to_all | solution.py:33
  233.6 5.6 %all-to-all-start.1 = ((bf16[128,2,7,2048]{3,1,2,0:T(2,128)(2,1)}), bf16[128,2,7,2048]{3,1,2,0:T(2,128)(2,1)}, u32[]{:S(2)}, u32[]{:S(2)}) async-start(bf16[128,2,7,2048]{3,1,2,0:T(2,128)(2,1)} %copy.48), calls=%async_computation.1 | async-start | bytes 14680064 | tf_op jit(solution)/shard_map/all_to_all | solution.py:75
  239.3 0.2 fusion.29
  239.6 2.6 reduce_sum.32
  242.2 86.7 %all-to-all-done.1 = bf16[128,2,7,2048]{3,1,2,0:T(2,128)(2,1)} async-done(((bf16[128,2,7,2048]{3,1,2,0:T(2,128)(2,1)}), bf16[128,2,7,2048]{3,1,2,0:T(2,128)(2,1)}, u32[]{:S(2)}, u32[]{:S(2)}) %all-to-all-start.1) | async-done | bytes 7340064 | tf_op jit(solution)/shard_map/all_to_all | solution.py:75
  328.9 11.4 %copy.49 = bf16[128,2,7,2048]{3,2,1,0:T(8,128)(2,1)} copy(bf16[128,2,7,2048]{3,1,2,0:T(2,128)(2,1)} %all-to-all-done.1) | data formatting | bytes 14680064 | tf_op jit(solution)/shard_map/all_to_all | solution.py:75
  340.2 10.7 %reshape.71 = bf16[1792,2048]{1,0:T(8,128)(2,1)} reshape(bf16[128,2,7,2048]{3,2,1,0:T(8,128)(2,1)} %copy.49) | data formatting | bytes 14680064 | tf_op jit(solution)/shard_map/reshape | solution.py:76
  350.9 14.9 %gather_fusion = bf16[1280,2048]{1,0:T(8,128)(2,1)} fusion(bf16[1792,2048]{1,0:T(8,128)(2,1)} %reshape.71, s32[2048]{0:T(1024)S(1)} %pad_clamp_fusion), kind=kCustom, calls=%fused_computation | custom fusion | bytes 10490880 | tf_op jit(solution)/shard_map/gather | solution.py:77
  365.8 10.6 %reshape.73 = f32[128,10,2048]{2,1,0:T(8,128)} reshape(bf16[1280,2048]{1,0:T(8,128)(2,1)} %gather_fusion) | data formatting | bytes 15728640 | tf_op jit(solution)/shard_map/convert_element_type | solution.py:79
  376.3 9.6 %multiply_reduce_fusion = f32[128,2048]{1,0:T(8,128)S(1)} fusion(f32[128,10,2048]{2,1,0:T(8,128)} %reshape.73, f32[128,10]{1,0:T(8,128)S(1)} %copy.50), kind=kLoop, calls=%fused_computation.2 | loop fusion | flops 4980736 | bytes 11539456 | tf_op jit(solution)/shard_map/reduce_sum | solution.py:79
  386.0 1.0 add_convert_fusion
  (30 shorter events, 1.0 us)
Async XLA Ops:
  0.0 90.3 %copy-start = (bf16[2,2048,128]{2,1,0:T(8,128)(2,1)S(1)}, bf16[2,2048,128]{2,1,0:T(8,128)(2,1)}, u32[]{:S(2)}) copy-start(bf16[2,2048,128]{2,1,0:T(8,128)(2,1)} %param.15) | copy-start | bytes 3145732
  0.0 7.5 %copy-start.4 = (s32[128,10]{0,1:T(8,128)S(1)}, s32[128,10]{0,1:T(8,128)}, u32[]{:S(2)}) copy-start(s32[128,10]{0,1:T(8,128)} %param.10) | copy-start | bytes 15364
  2.7 75.6 %all-to-all-start.2 = ((bf16[4,128,2048]{2,1,0:T(8,128)(2,1)}), bf16[4,128,2048]{2,1,0:T(8,128)(2,1)}, u32[]{:S(2)}, u32[]{:S(2)}) async-start(bf16[4,128,2048]{2,1,0:T(8,128)(2,1)} %broadcast_in_dim.8), calls=%async_computation.2 | async-start | bytes 4194304 | tf_op jit(solution)/shard_map/all_to_all | solution.py:17
  78.3 101.6 %all-to-all-start = ((bf16[128,2,7,2048]{3,1,2,0:T(2,128)(2,1)}), bf16[128,2,7,2048]{3,1,2,0:T(2,128)(2,1)}, u32[]{:S(2)}, u32[]{:S(2)}) async-start(bf16[128,2,7,2048]{3,1,2,0:T(2,128)(2,1)} %copy.45), calls=%async_computation | async-start | bytes 14680064 | tf_op jit(solution)/shard_map/all_to_all | solution.py:70
  90.3 2.7 copy-start.3
  179.9 53.7 %all-to-all-start.3 = ((f32[4,128,2048]{2,1,0:T(8,128)}), f32[4,128,2048]{2,1,0:T(8,128)}, u32[]{:S(2)}, u32[]{:S(2)}) async-start(f32[4,128,2048]{2,1,0:T(8,128)} %fusion.31), calls=%async_computation.3 | async-start | bytes 8388608 | tf_op jit(solution)/shard_map/all_to_all | solution.py:33
  228.4 10.7 %copy-start.5 = (s32[128,10]{0,1:T(8,128)S(1)}, s32[128,10]{0,1:T(8,128)}, u32[]{:S(2)}) copy-start(s32[128,10]{0,1:T(8,128)} %param.11) | copy-start | bytes 15364
  228.4 10.8 %copy-start.6 = (bf16[2048]{0:T(1024)(128)(2,1)S(1)}, bf16[2048]{0:T(1024)(128)(2,1)}, u32[]{:S(2)}) copy-start(bf16[2048]{0:T(1024)(128)(2,1)} %param.17) | copy-start | bytes 12292
  228.4 10.9 %copy-start.2 = (bf16[128,2048]{1,0:T(8,128)(2,1)S(1)}, bf16[128,2048]{1,0:T(8,128)(2,1)}, u32[]{:S(2)}) copy-start(bf16[128,2048]{1,0:T(8,128)(2,1)} %param.9) | copy-start | bytes 1572868
  233.6 95.3 %all-to-all-start.1 = ((bf16[128,2,7,2048]{3,1,2,0:T(2,128)(2,1)}), bf16[128,2,7,2048]{3,1,2,0:T(2,128)(2,1)}, u32[]{:S(2)}, u32[]{:S(2)}) async-start(bf16[128,2,7,2048]{3,1,2,0:T(2,128)(2,1)} %copy.48), calls=%async_computation.1 | async-start | bytes 14680064 | tf_op jit(solution)/shard_map/all_to_all | solution.py:75
  376.3 10.6 %copy-start.1 = (bf16[2,2048,128]{2,1,0:T(8,128)(2,1)S(1)}, bf16[2,2048,128]{2,1,0:T(8,128)(2,1)}, u32[]{:S(2)}) copy-start(bf16[2,2048,128]{2,1,0:T(8,128)(2,1)} %param.15) | copy-start | bytes 3145732
where the time goes:
time: 391 us; the launch traced here: 387 us
  waiting for transfers between devices  176 us (45%)
  local copies, waits for them, and re-layouts  135 us (35%)
  matrix products  34.4 us (9%)
  starting transfers between devices  27.2 us (7%)
  other arithmetic  14.3 us (4%)
    all_to_all x1, waiting for transfers between devices, on_device(): lax.all_to_all(produced, ('wide', 'narrow'), split_axis=0, concat_axis=0,...  86.7 us
    all_to_all x1, waiting for transfers between devices, on_device(): lax.all_to_all(outgoing, ('wide', 'narrow'), split_axis=0, concat_axis=0,...  84.2 us
    reshape x2, local copies, waits for them, and re-layouts, on_device(): outgoing = outgoing.reshape(devices, local_experts, CAP, model_width)  27.1 us
    scatter x1, local copies, waits for them, and re-layouts, on_device(): jnp.zeros((experts_total * CAP, model_width), jnp.bfloat16).at[slot_index]  25.6 us
    dot_general x1, matrix products, expert_block(): jnp.einsum('secf,efd->secd', hidden, w_down, preferred_element_type=jnp.f...  18.6 us
    gather x1, local copies, waits for them, and re-layouts, on_device(): returned[slot_index].reshape(tok_rows, top_count, model_width)  14.9 us
    convert_element_type x1, local copies, waits for them, and re-layouts, expert_block(): jnp.einsum('secf,efd->secd', hidden, w_down, preferred_element_type=jnp.f...  14.7 us
    all_to_all x1, starting transfers between devices, on_device(): lax.all_to_all(outgoing, ('wide', 'narrow'), split_axis=0, concat_axis=0,...  12 us
  transfers between devices with their start and end apart: 4, of which 3 were waited for; matrix products, arithmetic and copies ran while one was open for 32% of the time, Pallas kernels for 0%

commit v1 on v0

v1 whole, which is shorter than its diff:
```python
import functools

import jax
import jax.numpy as jnp
from jax import lax
from jax.experimental import pallas as pl
from jax.experimental.pallas import tpu as pltpu
from jax.sharding import PartitionSpec as P

CAP = 7
MESH = pl.DeviceIdType.MESH
F32 = jnp.float32
BF16 = jnp.bfloat16


def grid_of(wide):
    side = 1
    while 2 * side * side < wide:
        side *= 2
    return wide // (2 * side), side


def offsets(wide):
    zs, ys = grid_of(wide)
    steps = [(dz, dy, dc) for dz in range(zs) for dy in range(ys) for dc in range(2)]
    steps = steps[1:]

    def far(step):
        dz, dy, dc = step
        return min(dz, zs - dz) + min(dy, ys - dy)

    return sorted(steps, key=lambda s: (-far(s), (s[0] + 2 * s[1]) % 4, s[2]))


def silu_product(gate, up):
    return gate * (1.0 / (1.0 + jnp.exp(-gate))) * up


def kernel(
    cfg,
    tok, meta, wg, wu, wd, sgu, sd, gv,
    out,
    T, metas, D, DT, O, X, Y, Wg, Wu, Wd, acc, H, Sg, Sd, Gv, shared, part, rs_out, rs_in, own,
    m_send, m_recv, t_send, t_recv, d_send, d_recv, y_send, y_recv, r_send, r_recv, loc, w_sem,
    own_sem, yown_sem, s_sem,
):
    wide, narrow, chunks, n, rows, model, ff, hid, top = cfg
    zs, ys = grid_of(wide)
    w = lax.axis_index("wide")
    nx = lax.axis_index("narrow")
    steps = offsets(wide)
    lanes = narrow * rows
    slots = wide * 8

    def peer(step):
        dz, dy, dc = step
        core = w % 2
        y = (w // 2) % ys
        z = w // (2 * ys)
        return (((z + dz) % zs) * ys + (y + dy) % ys) * 2 + (core + dc) % 2

    def near(k):
        return (nx + k) % narrow

    barrier = pltpu.get_barrier_semaphore()
    for k in range(1, narrow):
        pl.semaphore_signal(barrier, inc=1, device_id=(w, near(k)), device_id_type=MESH)
    for step in steps:
        pl.semaphore_signal(barrier, inc=1, device_id=(peer(step), nx), device_id_type=MESH)

    def weight_copy(which, c):
        cols = pl.ds(c * n, n)
        source = (wg.at[:, cols, :], wu.at[:, cols, :], wd.at[:, :, cols])[which]
        return pltpu.make_async_copy(source, (Wg, Wu, Wd)[which].at[c], w_sem.at[which, c])

    def own_tokens(c):
        return pltpu.make_async_copy(tok.at[:, pl.ds(c * n, n)], T.at[c, nx], loc.at[c])

    def small(which):
        target = (Sg, Sd, Gv, metas.at[nx])[which]
        return pltpu.make_async_copy((sgu, sd, gv, meta)[which], target, s_sem.at[which])

    for which in range(4):
        small(which).start()
    for c in range(chunks):
        own_tokens(c).start()

    pl.semaphore_wait(barrier, narrow - 1 + len(steps))

    def meta_copy(k):
        return pltpu.make_async_remote_copy(
            meta, metas.at[nx], m_send.at[k - 1], m_recv.at[k - 1],
            device_id=(w, near(k)), device_id_type=MESH)

    def token_copy(c, k):
        return pltpu.make_async_remote_copy(
            tok.at[:, pl.ds(c * n, n)], T.at[c, nx], t_send.at[c, k - 1], t_recv.at[c, k - 1],
            device_id=(w, near(k)), device_id_type=MESH)

    for k in range(1, narrow):
        meta_copy(k).start()
    for c in range(chunks):
        for k in range(1, narrow):
            token_copy(c, k).start()
    for c in range(chunks):
        for which in range(3):
            weight_copy(which, c).start()

    small(3).wait()
    for k in range(1, narrow):
        meta_copy(k).wait_recv()
    pair = lax.broadcasted_iota(jnp.int32, (2 * wide, rows), 0)
    expert = (pair // 2) * (2 * narrow) + 2 * nx + pair % 2
    before = (
        lax.broadcasted_iota(jnp.int32, (rows, rows), 0)
        < lax.broadcasted_iota(jnp.int32, (rows, rows), 1)
    ).astype(F32).astype(BF16)
    rho = lax.broadcasted_iota(jnp.int32, (slots, 2 * wide), 0)
    col = lax.broadcasted_iota(jnp.int32, (slots, 2 * wide), 1)
    pos_parts, weight_parts = [], []
    for s in range(narrow):
        chosen = jnp.zeros((2 * wide, rows), F32)
        weight = jnp.zeros((2 * wide, rows), F32)
        for k in range(top):
            ids = jnp.broadcast_to(metas[s, k:k + 1, :], (2 * wide, rows))
            mix = jnp.broadcast_to(metas[s, top + k:top + k + 1, :], (2 * wide, rows))
            hit = ids == expert
            chosen = jnp.where(hit, 1.0, chosen)
            weight = jnp.where(hit, mix.astype(F32) * (1.0 / 256.0), weight)
        rank = jnp.dot(chosen.astype(BF16), before, preferred_element_type=F32)
        place = jnp.where(chosen > 0.5, rank + 1.0, 0.0).astype(BF16)
        spread = (
            (col == (rho // 8) * 2 + rho % 2) & ((rho % 8) // 2 == s)
        ).astype(F32).astype(BF16)
        pos_parts.append(jnp.dot(spread, place, preferred_element_type=F32))
        weight_parts.append(jnp.dot(spread, weight.astype(BF16), preferred_element_type=F32))
    pos8 = jnp.concatenate(pos_parts, axis=1)
    w8 = jnp.concatenate(weight_parts, axis=1)
    for j in range(CAP):
        D[j] = jnp.where(pos8 == j + 1.0, 1.0, 0.0).astype(BF16)

    def block_copy(c, step):
        to = peer(step)
        return pltpu.make_async_remote_copy(
            O.at[c, :, to], X.at[c, :, w], d_send.at[c], d_recv.at[c],
            device_id=(to, nx), device_id_type=MESH)

    def own_block(c):
        return pltpu.make_async_copy(O.at[c, :, w], X.at[c, :, w], own_sem.at[c])

    def dispatch(c, carry):
        own_tokens(c).wait()
        for k in range(1, narrow):
            token_copy(c, k).wait_recv()
        tokens = T[c].reshape(lanes, n)

        def one(j, carry):
            O[c, j] = jnp.dot(D[j], tokens, preferred_element_type=F32).reshape(
                wide, 8, n).astype(BF16)
            return carry

        lax.fori_loop(0, CAP, one, 0)
        for step in steps:
            block_copy(c, step).start()
        own_block(c).start()
        return carry

    lax.fori_loop(0, chunks, dispatch, 0)

    for which in range(3):
        small(which).wait()
    shared[...] = jnp.zeros_like(shared)

    def shared_step(c, carry):
        tokens = T[c].reshape(lanes, n)
        at = pl.ds(pl.multiple_of(c * n, n), n)
        shared[0] += jnp.dot(tokens, Sg[0, at, :], preferred_element_type=F32)
        shared[1] += jnp.dot(tokens, Sg[1, at, :], preferred_element_type=F32)
        shared[2] += jnp.dot(tokens, Gv[at, :], preferred_element_type=F32)
        return carry

    lax.fori_loop(0, chunks, shared_step, 0)
    shared_hidden = silu_product(shared[0], shared[1]).astype(BF16)
    shared[2] = 1.0 / (1.0 + jnp.exp(-shared[2]))
    posT, wT = pos8.T, w8.T
    for j in range(CAP):
        DT[j] = jnp.where(posT == j + 1.0, wT, 0.0).astype(BF16)

    parity = lax.broadcasted_iota(jnp.int32, (slots, n), 0) % 2
    first = jnp.where(parity == 0, 1.0, 0.0).astype(BF16)
    second = jnp.where(parity == 1, 1.0, 0.0).astype(BF16)

    def all_but_own(buf, sem):
        view = buf.at[:, pl.ds(0, wide - 1)]
        return pltpu.make_async_copy(view, view, sem)

    acc[...] = jnp.zeros_like(acc)

    def up_step(c, carry):
        weight_copy(0, c).wait()
        weight_copy(1, c).wait()
        own_block(c).wait()
        all_but_own(X.at[c], d_recv.at[c]).wait()
        gate_w = Wg[c].reshape(2 * n, ff)
        up_w = Wu[c].reshape(2 * n, ff)

        def one(j, carry):
            x = X[c, j].reshape(slots, n)
            both = jnp.concatenate([x * first, x * second], axis=1)
            acc[j, :, :ff] += jnp.dot(both, gate_w, preferred_element_type=F32)
            acc[j, :, ff:] += jnp.dot(both, up_w, preferred_element_type=F32)
            return carry

        lax.fori_loop(0, CAP, one, 0)
        return carry

    lax.fori_loop(0, chunks, up_step, 0)

    parity_h = lax.broadcasted_iota(jnp.int32, (slots, ff), 0) % 2

    def hidden(j, carry):
        h = silu_product(acc[j, :, :ff], acc[j, :, ff:])
        H[j, :, :ff] = jnp.where(parity_h == 0, h, 0.0).astype(BF16)
        H[j, :, ff:] = jnp.where(parity_h == 1, h, 0.0).astype(BF16)
        return carry

    lax.fori_loop(0, CAP, hidden, 0)

    def back_copy(c, step):
        to = peer(step)
        return pltpu.make_async_remote_copy(
            X.at[c, :, to], Y.at[c, :, w], y_send.at[c], y_recv.at[c],
            device_id=(to, nx), device_id_type=MESH)

    def own_back(c):
        return pltpu.make_async_copy(X.at[c, :, w], Y.at[c, :, w], yown_sem.at[c])

    def down_step(c, carry):
        weight_copy(2, c).wait()
        down_w = Wd[c].reshape(2 * ff, n)

        def one(j, carry):
            X[c, j] = jnp.dot(H[j], down_w, preferred_element_type=F32).reshape(
                wide, 8, n).astype(BF16)
            return carry

        lax.fori_loop(0, CAP, one, 0)
        for step in steps:
            back_copy(c, step).start()
        own_back(c).start()
        return carry

    lax.fori_loop(0, chunks, down_step, 0)

    def sum_copy(c, k):
        return pltpu.make_async_remote_copy(
            rs_out.at[c, near(k)], rs_in.at[c, nx], r_send.at[c, k - 1], r_recv.at[c, k - 1],
            device_id=(w, near(k)), device_id_type=MESH)

    def combine(c, carry):
        own_back(c).wait()
        all_but_own(Y.at[c], y_recv.at[c]).wait()
        at = pl.ds(pl.multiple_of(c * n, n), n)
        scale = jnp.concatenate([shared[2]] * (n // 128), axis=1)
        part[...] = scale * jnp.dot(shared_hidden, Sd[:, at], preferred_element_type=F32)

        def one(j, carry):
            part[...] += jnp.dot(DT[j], Y[c, j].reshape(slots, n), preferred_element_type=F32)
            return carry

        lax.fori_loop(0, CAP, one, 0)
        rs_out[c] = part[...].reshape(narrow, rows, n).astype(BF16)
        for k in range(1, narrow):
            sum_copy(c, k).start()
        mine = pl.ds(pl.multiple_of(nx * rows, rows), rows)
        own[c] = part[mine, :]
        return carry

    lax.fori_loop(0, chunks, combine, 0)

    for c in range(chunks):
        total = own[c]
        for k in range(1, narrow):
            sum_copy(c, k).wait_recv()
        for k in range(1, narrow):
            total = total + rs_in[c, near(k)].astype(F32)
        out[:, c * n:(c + 1) * n] = total.astype(BF16)

    for k in range(1, narrow):
        meta_copy(k).wait_send()

    def drain(c, carry):
        for k in range(1, narrow):
            token_copy(c, k).wait_send()
            sum_copy(c, k).wait_send()
        all_but_own(O.at[c], d_send.at[c]).wait()
        all_but_own(X.at[c], y_send.at[c]).wait()
        return carry

    lax.fori_loop(0, chunks, drain, 0)


def on_device(chunks, tokens, expert_ids, combine, w_gate, w_up, w_down, gate_up, down, gate_vec):
    rows, model = tokens.shape
    top = expert_ids.shape[1]
    wide, narrow = lax.axis_size("wide"), lax.axis_size("narrow")
    ff, hid = w_gate.shape[2], down.shape[0]
    n = model // chunks
    slots = wide * 8
    lanes = narrow * rows
    meta = jnp.concatenate([expert_ids.T, combine.T], axis=0)
    meta = jnp.pad(meta, ((0, -meta.shape[0] % 8), (0, 0)))
    gv = jnp.broadcast_to(gate_vec[:, None], (model, 128))
    cfg = (wide, narrow, chunks, n, rows, model, ff, hid, top)
    any_spec = pl.BlockSpec(memory_space=pl.ANY)
    dma = pltpu.SemaphoreType.DMA
    return pl.pallas_call(
        functools.partial(kernel, cfg),
        out_shape=jax.ShapeDtypeStruct((rows, model), BF16),
        in_specs=[any_spec] * 8,
        out_specs=pl.BlockSpec(memory_space=pltpu.VMEM),
        scratch_shapes=[
            pltpu.VMEM((chunks, narrow, rows, n), BF16),
            pltpu.VMEM((narrow, *meta.shape), jnp.int32),
            pltpu.VMEM((CAP, slots, lanes), BF16),
            pltpu.VMEM((CAP, lanes, slots), BF16),
            pltpu.VMEM((chunks, CAP, wide, 8, n), BF16),
            pltpu.VMEM((chunks, CAP, wide, 8, n), BF16),
            pltpu.VMEM((chunks, CAP, wide, 8, n), BF16),
            pltpu.VMEM((chunks, 2, n, ff), BF16),
            pltpu.VMEM((chunks, 2, n, ff), BF16),
            pltpu.VMEM((chunks, 2, ff, n), BF16),
            pltpu.VMEM((CAP, slots, 2 * ff), F32),
            pltpu.VMEM((CAP, slots, 2 * ff), BF16),
            pltpu.VMEM((2, model, hid), BF16),
            pltpu.VMEM((hid, model), BF16),
            pltpu.VMEM((model, 128), BF16),
            pltpu.VMEM((3, lanes, hid), F32),
            pltpu.VMEM((lanes, n), F32),
            pltpu.VMEM((chunks, narrow, rows, n), BF16),
            pltpu.VMEM((chunks, narrow, rows, n), BF16),
            pltpu.VMEM((chunks, rows, n), F32),
            dma((narrow - 1,)), dma((narrow - 1,)),
            dma((chunks, narrow - 1)), dma((chunks, narrow - 1)),
            dma((chunks,)), dma((chunks,)),
            dma((chunks,)), dma((chunks,)),
            dma((chunks, narrow - 1)), dma((chunks, narrow - 1)),
            dma((chunks,)), dma((3, chunks)),
            dma((chunks,)), dma((chunks,)), dma((4,)),
        ],
        compiler_params=pltpu.CompilerParams(
            collective_id=0, has_side_effects=True, vmem_limit_bytes=66 * 1000 * 1000),
    )(tokens, meta, w_gate, w_up, w_down, gate_up, down, gv)


def solution(mesh, chunks=4):
    return jax.shard_map(
        functools.partial(on_device, chunks),
        mesh=mesh,
        in_specs=(
            P(("wide", "narrow"), None),
            P(("wide", "narrow"), None),
            P(("wide", "narrow"), None),
            P(("wide", "narrow"), None, None),
            P(("wide", "narrow"), None, None),
            P(("wide", "narrow"), None, None),
            P(None, None, "narrow"),
            P("narrow", None),
            P(),
        ),
        out_specs=P(("wide", "narrow"), None),
        check_vma=False,
    )
```

time: 391 us -> 224 us (0.57)
  Pallas kernels: 0 us -> 216 us
  waiting for transfers between devices: 176 us -> 0 us
  local copies, waits for them, and re-layouts: 135 us -> 4.3 us
  matrix products: 34.4 us -> 0 us
  starting transfers between devices: 27.2 us -> 0 us
  other arithmetic: 14.3 us -> 0.72 us
    pallas_call x0 -> x1, Pallas kernels: none -> 216 us  [on_device(): pl.pallas_call(functools.partial(kernel, cfg), out_shape=jax.ShapeDtypeSt...]
    all_to_all x4 -> x0, waiting for transfers between devices: 176 us -> none  [the longest x1 86.7 us: on_device(): lax.all_to_all(produced, ('wide', 'narrow'), split_axis=0, concat_axis=0,...]
    reshape x4 -> x0, local copies, waits for them, and re-layouts: 47.6 us -> none  [the longest x2 27.1 us: on_device(): outgoing = outgoing.reshape(devices, local_experts, CAP, model_width)]
    dot_general x5 -> x0, matrix products: 34.4 us -> none  [the longest x1 18.6 us: expert_block(): jnp.einsum('secf,efd->secd', hidden, w_down, preferred_element_type=jnp.f...]
    all_to_all x4 -> x0, starting transfers between devices: 27.2 us -> none  [the longest x1 12 us: on_device(): lax.all_to_all(outgoing, ('wide', 'narrow'), split_axis=0, concat_axis=0,...]
    scatter x1 -> x0, local copies, waits for them, and re-layouts: 25.6 us -> none  [on_device(): jnp.zeros((experts_total * CAP, model_width), jnp.bfloat16).at[slot_index]]
    convert_element_type x2 -> x0, local copies, waits for them, and re-layouts: 25.2 us -> none  [the longest x1 14.7 us: expert_block(): jnp.einsum('secf,efd->secd', hidden, w_down, preferred_element_type=jnp.f...]
    gather x1 -> x0, local copies, waits for them, and re-layouts: 14.9 us -> none  [on_device(): returned[slot_index].reshape(tok_rows, top_count, model_width)]
  transfers between devices with their start and end apart: 4 -> 0, of which waited for: 3 -> 0; matrix products, arithmetic and copies ran while one was open for 32% -> 0% of each run, Pallas kernels for 0% -> 0%
where the time goes in v1:
time: 224 us; the launch traced here: 221 us
  Pallas kernels  216 us (96%)
  local copies, waits for them, and re-layouts  4.3 us (2%)
    pallas_call x1, Pallas kernels, on_device(): pl.pallas_call(functools.partial(kernel, cfg), out_shape=jax.ShapeDtypeSt...  216 us

profile of v1, /device:TPU:1, one launch (start us, length us, event | category | flops | bytes accessed | tf_op | source)
XLA Modules:
  0.0 221.1 jit_solution(16368249210899737061)
XLA Ops:
  0.0 0.7 pad_add_fusion
  0.7 0.6 pad.4.meta
  1.3 1.8 broadcast_in_dim.2.gv
  3.1 216.1 %shard_map.91 = bf16[128,2048]{1,0:T(8,128)(2,1)} custom-call(bf16[128,2048]{1,0:T(8,128)(2,1)} %tok.1, s32[24,128]{1,0:T(8,128)} %pad.4.meta, bf16[2,2048,512]{2,1,0:T(8,128)(2,1)} %wg.1, bf16[2,2048,512]{2,1,0:T(8,128)(2,1)} %wu.1, bf16[2,512,2048]{2,1,0:T(8,128)(2,1)} %wd.1, bf16[2,2048,128]{2,1,0:T(8,128)(2,1)} %sgu.1, bf16[128,2048]{1,0:T(8,128)(2,1)} %sd.1, ...), custom_call_target="tpu_custom_call" | custom-call | tf_op jit(solution)/shard_map/pallas_call | solution.py:317
  219.3 1.9 copy.11

commit v2 on v1

--- a/solution.py
+++ b/solution.py
@@ -38,9 +38,9 @@
 
 def kernel(
     cfg,
-    tok, meta, wg, wu, wd, sgu, sd, gv,
+    tok, ids_in, mix_in, wg, wu, wd, sgu, sd, gv,
     out,
-    T, metas, D, DT, O, X, Y, Wg, Wu, Wd, acc, H, Sg, Sd, Gv, shared, part, rs_out, rs_in, own,
+    T, idv, mixv, D, DT, O, X, Y, Wg, Wu, Wd, acc, H, Sg, Sd, Gv, shared, part, rs_out, rs_in, own,
     m_send, m_recv, t_send, t_recv, d_send, d_recv, y_send, y_recv, r_send, r_recv, loc, w_sem,
     own_sem, yown_sem, s_sem,
 ):
@@ -77,19 +77,20 @@
         return pltpu.make_async_copy(tok.at[:, pl.ds(c * n, n)], T.at[c, nx], loc.at[c])
 
     def small(which):
-        target = (Sg, Sd, Gv, metas.at[nx])[which]
-        return pltpu.make_async_copy((sgu, sd, gv, meta)[which], target, s_sem.at[which])
-
-    for which in range(4):
+        target = (Sg, Sd, Gv, idv.at[nx], mixv.at[nx])[which]
+        return pltpu.make_async_copy((sgu, sd, gv, ids_in, mix_in)[which], target, s_sem.at[which])
+
+    for which in range(5):
         small(which).start()
     for c in range(chunks):
         own_tokens(c).start()
 
     pl.semaphore_wait(barrier, narrow - 1 + len(steps))
 
-    def meta_copy(k):
-        return pltpu.make_async_remote_copy(
-            meta, metas.at[nx], m_send.at[k - 1], m_recv.at[k - 1],
+    def meta_copy(which, k):
+        source, target = ((ids_in, idv), (mix_in, mixv))[which]
+        return pltpu.make_async_remote_copy(
+            source, target.at[nx], m_send.at[which, k - 1], m_recv.at[which, k - 1],
             device_id=(w, near(k)), device_id_type=MESH)
 
     def token_copy(c, k):
@@ -98,7 +99,8 @@
             device_id=(w, near(k)), device_id_type=MESH)
 
     for k in range(1, narrow):
-        meta_copy(k).start()
+        meta_copy(0, k).start()
+        meta_copy(1, k).start()
     for c in range(chunks):
         for k in range(1, narrow):
             token_copy(c, k).start()
@@ -107,37 +109,44 @@
             weight_copy(which, c).start()
 
     small(3).wait()
+    small(4).wait()
     for k in range(1, narrow):
-        meta_copy(k).wait_recv()
+        meta_copy(0, k).wait_recv()
+        meta_copy(1, k).wait_recv()
     pair = lax.broadcasted_iota(jnp.int32, (2 * wide, rows), 0)
     expert = (pair // 2) * (2 * narrow) + 2 * nx + pair % 2
     before = (
         lax.broadcasted_iota(jnp.int32, (rows, rows), 0)
         < lax.broadcasted_iota(jnp.int32, (rows, rows), 1)
     ).astype(F32).astype(BF16)
-    rho = lax.broadcasted_iota(jnp.int32, (slots, 2 * wide), 0)
-    col = lax.broadcasted_iota(jnp.int32, (slots, 2 * wide), 1)
-    pos_parts, weight_parts = [], []
+    rho = lax.broadcasted_iota(jnp.int32, (slots, wide * 2), 0)
+    col = lax.broadcasted_iota(jnp.int32, (slots, wide * 2), 1)
+    pos_parts, weight_parts = [[], []], [[], []]
     for s in range(narrow):
         chosen = jnp.zeros((2 * wide, rows), F32)
         weight = jnp.zeros((2 * wide, rows), F32)
         for k in range(top):
-            ids = jnp.broadcast_to(metas[s, k:k + 1, :], (2 * wide, rows))
-            mix = jnp.broadcast_to(metas[s, top + k:top + k + 1, :], (2 * wide, rows))
+            ids = jnp.broadcast_to(idv[s, k:k + 1, :], (2 * wide, rows))
+            mix = jnp.broadcast_to(mixv[s, k:k + 1, :], (2 * wide, rows))
             hit = ids == expert
             chosen = jnp.where(hit, 1.0, chosen)
             weight = jnp.where(hit, mix.astype(F32) * (1.0 / 256.0), weight)
         rank = jnp.dot(chosen.astype(BF16), before, preferred_element_type=F32)
         place = jnp.where(chosen > 0.5, rank + 1.0, 0.0).astype(BF16)
-        spread = (
-            (col == (rho // 8) * 2 + rho % 2) & ((rho % 8) // 2 == s)
-        ).astype(F32).astype(BF16)
-        pos_parts.append(jnp.dot(spread, place, preferred_element_type=F32))
-        weight_parts.append(jnp.dot(spread, weight.astype(BF16), preferred_element_type=F32))
-    pos8 = jnp.concatenate(pos_parts, axis=1)
-    w8 = jnp.concatenate(weight_parts, axis=1)
-    for j in range(CAP):
-        D[j] = jnp.where(pos8 == j + 1.0, 1.0, 0.0).astype(BF16)
+        weight = weight.astype(BF16)
+        for e in range(2):
+            spread = ((col == (rho // 8) * 2 + e) & (rho % 4 == s)).astype(F32).astype(BF16)
+            pos_parts[e].append(jnp.dot(spread, place, preferred_element_type=F32))
+            weight_parts[e].append(jnp.dot(spread, weight, preferred_element_type=F32))
+    half = (lax.broadcasted_iota(jnp.int32, (slots, lanes), 0) % 8) // 4
+    pos, mixes = [], []
+    for e in range(2):
+        found = jnp.concatenate(pos_parts[e], axis=1)
+        pos.append(jnp.where(found > 0.5, found - half.astype(F32), -9.0))
+        mixes.append(jnp.concatenate(weight_parts[e], axis=1))
+    for g in range(CAP):
+        D[g * slots:(g + 1) * slots, :] = jnp.where(
+            (pos[0] == 2.0 * g + 1.0) | (pos[1] == 2.0 * g - 6.0), 1.0, 0.0).astype(BF16)
 
     def block_copy(c, step):
         to = peer(step)
@@ -154,12 +163,8 @@
             token_copy(c, k).wait_recv()
         tokens = T[c].reshape(lanes, n)
 
-        def one(j, carry):
-            O[c, j] = jnp.dot(D[j], tokens, preferred_element_type=F32).reshape(
-                wide, 8, n).astype(BF16)
-            return carry
-
-        lax.fori_loop(0, CAP, one, 0)
+        O[c] = jnp.dot(D[...], tokens, preferred_element_type=F32).reshape(
+            CAP, wide, 8, n).astype(BF16)
         for step in steps:
             block_copy(c, step).start()
         own_block(c).start()
@@ -176,19 +181,20 @@
         at = pl.ds(pl.multiple_of(c * n, n), n)
         shared[0] += jnp.dot(tokens, Sg[0, at, :], preferred_element_type=F32)
         shared[1] += jnp.dot(tokens, Sg[1, at, :], preferred_element_type=F32)
-        shared[2] += jnp.dot(tokens, Gv[at, :], preferred_element_type=F32)
+        scored = tokens.astype(F32) * Gv[:, at].astype(F32)
+        for q in range(n // 128):
+            shared[2] += scored[:, q * 128:(q + 1) * 128]
         return carry
 
     lax.fori_loop(0, chunks, shared_step, 0)
     shared_hidden = silu_product(shared[0], shared[1]).astype(BF16)
-    shared[2] = 1.0 / (1.0 + jnp.exp(-shared[2]))
-    posT, wT = pos8.T, w8.T
-    for j in range(CAP):
-        DT[j] = jnp.where(posT == j + 1.0, wT, 0.0).astype(BF16)
-
-    parity = lax.broadcasted_iota(jnp.int32, (slots, n), 0) % 2
-    first = jnp.where(parity == 0, 1.0, 0.0).astype(BF16)
-    second = jnp.where(parity == 1, 1.0, 0.0).astype(BF16)
+    score = jnp.broadcast_to(jnp.sum(shared[2], axis=1, keepdims=True), (lanes, 128))
+    shared[2] = 1.0 / (1.0 + jnp.exp(-score))
+    pos_t, mix_t = [p.T for p in pos], [m.T for m in mixes]
+    for g in range(CAP):
+        DT[:, g * slots:(g + 1) * slots] = (
+            jnp.where(pos_t[0] == 2.0 * g + 1.0, mix_t[0], 0.0)
+            + jnp.where(pos_t[1] == 2.0 * g - 6.0, mix_t[1], 0.0)).astype(BF16)
 
     def all_but_own(buf, sem):
         view = buf.at[:, pl.ds(0, wide - 1)]
@@ -201,30 +207,30 @@
         weight_copy(1, c).wait()
         own_block(c).wait()
         all_but_own(X.at[c], d_recv.at[c]).wait()
-        gate_w = Wg[c].reshape(2 * n, ff)
-        up_w = Wu[c].reshape(2 * n, ff)
-
-        def one(j, carry):
-            x = X[c, j].reshape(slots, n)
-            both = jnp.concatenate([x * first, x * second], axis=1)
-            acc[j, :, :ff] += jnp.dot(both, gate_w, preferred_element_type=F32)
-            acc[j, :, ff:] += jnp.dot(both, up_w, preferred_element_type=F32)
+
+        def one(e, carry):
+            x = X[c, pl.ds(3 * e, 4)].reshape(4 * slots, n)
+            acc[e, :, :ff] += jnp.dot(x, Wg[c, e], preferred_element_type=F32)
+            acc[e, :, ff:] += jnp.dot(x, Wu[c, e], preferred_element_type=F32)
             return carry
 
-        lax.fori_loop(0, CAP, one, 0)
+        lax.fori_loop(0, 2, one, 0)
         return carry
 
     lax.fori_loop(0, chunks, up_step, 0)
 
-    parity_h = lax.broadcasted_iota(jnp.int32, (slots, ff), 0) % 2
-
-    def hidden(j, carry):
-        h = silu_product(acc[j, :, :ff], acc[j, :, ff:])
-        H[j, :, :ff] = jnp.where(parity_h == 0, h, 0.0).astype(BF16)
-        H[j, :, ff:] = jnp.where(parity_h == 1, h, 0.0).astype(BF16)
-        return carry
-
-    lax.fori_loop(0, CAP, hidden, 0)
+    upper = (lax.broadcasted_iota(jnp.int32, (slots, ff), 0) % 8) // 4
+
+    def hidden(g, carry):
+        e, r = g // 4, g % 4
+        at = pl.ds(pl.multiple_of(r * slots, slots), slots)
+        h = silu_product(acc[e, at, :ff], acc[e, at, ff:])
+        shared_row = (g == 3).astype(jnp.int32) - (g == 4).astype(jnp.int32)
+        keep = shared_row * (2 * upper - 1) <= 0
+        H[e, at, :] = jnp.where(keep, h, 0.0).astype(BF16)
+        return carry
+
+    lax.fori_loop(0, 8, hidden, 0)
 
     def back_copy(c, step):
         to = peer(step)
@@ -237,14 +243,11 @@
 
     def down_step(c, carry):
         weight_copy(2, c).wait()
-        down_w = Wd[c].reshape(2 * ff, n)
-
-        def one(j, carry):
-            X[c, j] = jnp.dot(H[j], down_w, preferred_element_type=F32).reshape(
-                wide, 8, n).astype(BF16)
-            return carry
-
-        lax.fori_loop(0, CAP, one, 0)
+        low = jnp.dot(H[0], Wd[c, 0], preferred_element_type=F32)
+        high = jnp.dot(H[1], Wd[c, 1], preferred_element_type=F32)
+        X[c, 0:3] = low[:3 * slots].reshape(3, wide, 8, n).astype(BF16)
+        X[c, 3] = (low[3 * slots:] + high[:slots]).reshape(wide, 8, n).astype(BF16)
+        X[c, 4:7] = high[slots:].reshape(3, wide, 8, n).astype(BF16)
         for step in steps:
             back_copy(c, step).start()
         own_back(c).start()
@@ -262,13 +265,8 @@
         all_but_own(Y.at[c], y_recv.at[c]).wait()
         at = pl.ds(pl.multiple_of(c * n, n), n)
         scale = jnp.concatenate([shared[2]] * (n // 128), axis=1)
-        part[...] = scale * jnp.dot(shared_hidden, Sd[:, at], preferred_element_type=F32)
-
-        def one(j, carry):
-            part[...] += jnp.dot(DT[j], Y[c, j].reshape(slots, n), preferred_element_type=F32)
-            return carry
-
-        lax.fori_loop(0, CAP, one, 0)
+        part[...] = scale * jnp.dot(shared_hidden, Sd[:, at], preferred_element_type=F32) + jnp.dot(
+            DT[...], Y[c].reshape(CAP * slots, n), preferred_element_type=F32)
         rs_out[c] = part[...].reshape(narrow, rows, n).astype(BF16)
         for k in range(1, narrow):
             sum_copy(c, k).start()
@@ -287,7 +285,8 @@
         out[:, c * n:(c + 1) * n] = total.astype(BF16)
 
     for k in range(1, narrow):
-        meta_copy(k).wait_send()
+        meta_copy(0, k).wait_send()
+        meta_copy(1, k).wait_send()
 
     def drain(c, carry):
         for k in range(1, narrow):
@@ -308,52 +307,51 @@
     n = model // chunks
     slots = wide * 8
     lanes = narrow * rows
-    meta = jnp.concatenate([expert_ids.T, combine.T], axis=0)
-    meta = jnp.pad(meta, ((0, -meta.shape[0] % 8), (0, 0)))
-    gv = jnp.broadcast_to(gate_vec[:, None], (model, 128))
     cfg = (wide, narrow, chunks, n, rows, model, ff, hid, top)
     any_spec = pl.BlockSpec(memory_space=pl.ANY)
     dma = pltpu.SemaphoreType.DMA
     return pl.pallas_call(
         functools.partial(kernel, cfg),
         out_shape=jax.ShapeDtypeStruct((rows, model), BF16),
-        in_specs=[any_spec] * 8,
+        in_specs=[any_spec] * 9,
         out_specs=pl.BlockSpec(memory_space=pltpu.VMEM),
         scratch_shapes=[
             pltpu.VMEM((chunks, narrow, rows, n), BF16),
-            pltpu.VMEM((narrow, *meta.shape), jnp.int32),
-            pltpu.VMEM((CAP, slots, lanes), BF16),
-            pltpu.VMEM((CAP, lanes, slots), BF16),
+            pltpu.VMEM((narrow, top, rows), jnp.int32),
+            pltpu.VMEM((narrow, top, rows), jnp.int32),
+            pltpu.VMEM((CAP * slots, lanes), BF16),
+            pltpu.VMEM((lanes, CAP * slots), BF16),
             pltpu.VMEM((chunks, CAP, wide, 8, n), BF16),
             pltpu.VMEM((chunks, CAP, wide, 8, n), BF16),
             pltpu.VMEM((chunks, CAP, wide, 8, n), BF16),
             pltpu.VMEM((chunks, 2, n, ff), BF16),
             pltpu.VMEM((chunks, 2, n, ff), BF16),
             pltpu.VMEM((chunks, 2, ff, n), BF16),
-            pltpu.VMEM((CAP, slots, 2 * ff), F32),
-            pltpu.VMEM((CAP, slots, 2 * ff), BF16),
+            pltpu.VMEM((2, 4 * slots, 2 * ff), F32),
+            pltpu.VMEM((2, 4 * slots, ff), BF16),
             pltpu.VMEM((2, model, hid), BF16),
             pltpu.VMEM((hid, model), BF16),
-            pltpu.VMEM((model, 128), BF16),
+            pltpu.VMEM((1, model), BF16),
             pltpu.VMEM((3, lanes, hid), F32),
             pltpu.VMEM((lanes, n), F32),
             pltpu.VMEM((chunks, narrow, rows, n), BF16),
             pltpu.VMEM((chunks, narrow, rows, n), BF16),
             pltpu.VMEM((chunks, rows, n), F32),
-            dma((narrow - 1,)), dma((narrow - 1,)),
+            dma((2, narrow - 1)), dma((2, narrow - 1)),
             dma((chunks, narrow - 1)), dma((chunks, narrow - 1)),
             dma((chunks,)), dma((chunks,)),
             dma((chunks,)), dma((chunks,)),
             dma((chunks, narrow - 1)), dma((chunks, narrow - 1)),
             dma((chunks,)), dma((3, chunks)),
-            dma((chunks,)), dma((chunks,)), dma((4,)),
+            dma((chunks,)), dma((chunks,)), dma((5,)),
         ],
         compiler_params=pltpu.CompilerParams(
             collective_id=0, has_side_effects=True, vmem_limit_bytes=66 * 1000 * 1000),
-    )(tokens, meta, w_gate, w_up, w_down, gate_up, down, gv)
-
-
-def solution(mesh, chunks=4):
+    )(tokens, expert_ids.T, combine.T, w_gate, w_up, w_down, gate_up, down,
+      gate_vec.reshape(1, model))
+
+
+def solution(mesh, chunks=16):
     return jax.shard_map(
         functools.partial(on_device, chunks),
         mesh=mesh,

time: 224 us -> 192 us (0.86); the launches traced: 221 us -> 192 us
  Pallas kernels: 216 us -> 188 us
    pallas_call x1, Pallas kernels: 216 us -> 188 us  [on_device(): pl.pallas_call(functools.partial(kernel, cfg), out_shape=jax.ShapeDtypeSt...]
where the time goes in v2:
time: 192 us
  Pallas kernels  188 us (98%)
  local copies, waits for them, and re-layouts  3.17 us (2%)
    pallas_call x1, Pallas kernels, on_device(): pl.pallas_call(functools.partial(kernel, cfg), out_shape=jax.ShapeDtypeSt...  188 us

profile of v2, /device:TPU:1, one launch (start us, length us, event | category | flops | bytes accessed | tf_op | source)
XLA Modules:
  0.0 191.6 jit_solution(7496699275678678876)
XLA Ops:
  0.0 1.3 reshape.3.gv
  1.3 188.4 %shard_map.91 = bf16[128,2048]{1,0:T(8,128)(2,1)} custom-call(bf16[128,2048]{1,0:T(8,128)(2,1)} %tok.1, s32[10,128]{1,0:T(8,128)} %bitcast.2, s32[10,128]{1,0:T(8,128)} %bitcast.3, bf16[2,2048,512]{2,1,0:T(8,128)(2,1)} %wg.1, bf16[2,2048,512]{2,1,0:T(8,128)(2,1)} %wu.1, bf16[2,512,2048]{2,1,0:T(8,128)(2,1)} %wd.1, bf16[2,2048,128]{2,1,0:T(8,128)(2,1)} %sgu.1, ...), custom_call_target="tpu_custom_call" | custom-call | tf_op jit(solution)/shard_map/pallas_call | solution.py:313
  189.7 1.9 copy.11

commit v3 on v0

v3 whole, which is shorter than its diff:
```python
import functools

import jax
import jax.numpy as jnp
from jax import lax
from jax.experimental import pallas as pl
from jax.experimental.pallas import tpu as pltpu
from jax.sharding import PartitionSpec as P

CAP = 7
MESH = pl.DeviceIdType.MESH
F32 = jnp.float32
BF16 = jnp.bfloat16


SIDE = 4
GROUP = 2 * SIDE * SIDE
KINDS = (0, 1, 0, 2)


def offsets():
    steps = [(da, db, dc) for da in range(SIDE) for db in range(SIDE) for dc in range(2)]
    steps = steps[1:]

    def far(step):
        return min(step[0], SIDE - step[0]) + min(step[1], SIDE - step[1])

    return sorted(steps, key=lambda s: (-far(s), (s[0] + 2 * s[1]) % 4, s[2]))


def silu_product(gate, up):
    return gate * (1.0 / (1.0 + jnp.exp(-gate))) * up


def kernel(
    cfg,
    tok, ids_in, mix_in, wg, wu, wd, sgu, sd, gv,
    out,
    T, TO, idv, mixv, D, O, X, Y, Wg, Wu, Wd, acc, H, Sg, Sd, Gv, shared, rs_out, rs_in,
    sh_out, sh_in, own,
    m_send, m_recv, t_send, t_recv, to_send, to_recv, d_send, d_recv, y_send, y_recv,
    r_send, r_recv, s_send, s_recv, loc, loco, w_sem, own_sem, yown_sem, small_sem,
):
    chunks, n, rows, model, ff, hid, top = cfg
    w = lax.axis_index("wide")
    x = lax.axis_index("narrow")
    core, y, z = w % 2, (w // 2) % SIDE, w // (2 * SIDE)
    at = (x, y, z)
    rounds, pairs = chunks // 4, chunks // 2
    lanes = SIDE * rows
    slots = GROUP * 8
    steps = offsets()

    def device(xx, yy, zz, cc):
        return ((zz * SIDE + yy) * 2 + cc, xx)

    def place(p):
        first, second = ((z, y), (z, x), (x, y))[p]
        return (first * SIDE + second) * 2 + core

    def far_peer(p, step):
        da, db, dc = step
        first, second = ((z, y), (z, x), (x, y))[p]
        first, second, cc = (first + da) % SIDE, (second + db) % SIDE, (core + dc) % 2
        spot = ((x, second, first), (second, y, first), (first, second, z))[p]
        return (first * SIDE + second) * 2 + cc, device(*spot, cc)

    def near(p, k):
        other = (at[p] + k) % SIDE
        spot = tuple(other if q == p else at[q] for q in range(3))
        return other, device(*spot, core)

    barrier = pltpu.get_barrier_semaphore()
    greeted = 0
    for dx in range(SIDE):
        for dy in range(SIDE):
            for dz in range(SIDE):
                for dc in range(2):
                    if dx * dy * dz == 0 and (dx, dy, dz, dc) != (0, 0, 0, 0):
                        greeted += 1
                        pl.semaphore_signal(
                            barrier, inc=1,
                            device_id=device((x + dx) % SIDE, (y + dy) % SIDE, (z + dz) % SIDE,
                                             (core + dc) % 2),
                            device_id_type=MESH)

    def weight_copy(which, m):
        cols = pl.ds(m * 2 * n, 2 * n)
        source = (wg.at[:, cols, :], wu.at[:, cols, :], wd.at[:, :, cols])[which]
        return pltpu.make_async_copy(source, (Wg, Wu, Wd)[which].at[m], w_sem.at[which, m])

    def own_tokens(c):
        return pltpu.make_async_copy(tok.at[:, pl.ds(c * n, n)], T.at[c, x], loc.at[c])

    def own_tokens_other(p, r):
        c = r * 4 + KINDS.index(p)
        return pltpu.make_async_copy(
            tok.at[:, pl.ds(c * n, n)], TO.at[p - 1, r, at[p]], loco.at[p - 1, r])

    def small(which):
        source = (sgu, sd, gv)[which]
        return pltpu.make_async_copy(source, (Sg, Sd, Gv)[which], small_sem.at[which])

    def own_meta(which, p):
        source, target = ((ids_in, idv), (mix_in, mixv))[which]
        return pltpu.make_async_copy(
            source, target.at[p, at[p]], small_sem.at[3 + which * 3 + p])

    for p in range(3):
        own_meta(0, p).start()
        own_meta(1, p).start()
    for c in range(chunks):
        own_tokens(c).start()
    for r in range(rounds):
        own_tokens_other(1, r).start()
        own_tokens_other(2, r).start()
    for which in range(3):
        small(which).start()

    pl.semaphore_wait(barrier, greeted)

    def meta_copy(which, p, k):
        source, target = ((ids_in, idv), (mix_in, mixv))[which]
        return pltpu.make_async_remote_copy(
            source, target.at[p, at[p]], m_send.at[which, p, k - 1], m_recv.at[which, p, k - 1],
            device_id=near(p, k)[1], device_id_type=MESH)

    def token_copy(c, k):
        return pltpu.make_async_remote_copy(
            tok.at[:, pl.ds(c * n, n)], T.at[c, x], t_send.at[c, k - 1], t_recv.at[c, k - 1],
            device_id=near(0, k)[1], device_id_type=MESH)

    def token_copy_other(p, r, k):
        c = r * 4 + KINDS.index(p)
        return pltpu.make_async_remote_copy(
            tok.at[:, pl.ds(c * n, n)], TO.at[p - 1, r, at[p]],
            to_send.at[p - 1, r, k - 1], to_recv.at[p - 1, r, k - 1],
            device_id=near(p, k)[1], device_id_type=MESH)

    for p in range(3):
        for k in range(1, SIDE):
            meta_copy(0, p, k).start()
            meta_copy(1, p, k).start()
    for r in range(rounds):
        for q, p in enumerate(KINDS):
            for k in range(1, SIDE):
                if p == 0:
                    token_copy(r * 4 + q, k).start()
                else:
                    token_copy_other(p, r, k).start()
    for m in range(pairs):
        for which in range(3):
            weight_copy(which, m).start()

    for p in range(3):
        for which in range(2):
            own_meta(which, p).wait()
            for k in range(1, SIDE):
                meta_copy(which, p, k).wait_recv()
    pair = lax.broadcasted_iota(jnp.int32, (2 * GROUP, rows), 0)
    before = (
        lax.broadcasted_iota(jnp.int32, (rows, rows), 0)
        < lax.broadcasted_iota(jnp.int32, (rows, rows), 1)
    ).astype(F32).astype(BF16)
    rho = lax.broadcasted_iota(jnp.int32, (slots, 2 * GROUP), 0)
    col = lax.broadcasted_iota(jnp.int32, (slots, 2 * GROUP), 1)
    half = ((lax.broadcasted_iota(jnp.int32, (slots, lanes), 0) % 8) // 4).astype(F32)

    def slot_tables(p):
        by_first = jnp.where(p == 2, 2, 64)
        by_second = jnp.where(p == 1, 2, 16)
        base = jnp.where(p == 0, 2 * x, jnp.where(p == 1, 16 * y, 64 * z))
        expert = (
            base + (pair // 16) * by_first + ((pair // 4) % 4) * by_second
            + ((pair // 2) % 2) * 8 + pair % 2)
        pos_parts, weight_parts = [[], []], [[], []]
        for s in range(SIDE):
            chosen = jnp.zeros((2 * GROUP, rows), F32)
            weight = jnp.zeros((2 * GROUP, rows), F32)
            for k in range(top):
                ids = jnp.broadcast_to(idv[p, s, k:k + 1, :], (2 * GROUP, rows))
                mix = jnp.broadcast_to(mixv[p, s, k:k + 1, :], (2 * GROUP, rows))
                hit = ids == expert
                chosen = jnp.where(hit, 1.0, chosen)
                weight = jnp.where(hit, mix.astype(F32) * (1.0 / 256.0), weight)
            rank = jnp.dot(chosen.astype(BF16), before, preferred_element_type=F32)
            spot = jnp.where(chosen > 0.5, rank + 1.0, 0.0).astype(BF16)
            weight = weight.astype(BF16)
            for e in range(2):
                spread = ((col == (rho // 8) * 2 + e) & (rho % 4 == s)).astype(F32).astype(BF16)
                pos_parts[e].append(jnp.dot(spread, spot, preferred_element_type=F32))
                weight_parts[e].append(jnp.dot(spread, weight, preferred_element_type=F32))
        pos, mixes = [], []
        for e in range(2):
            found = jnp.concatenate(pos_parts[e], axis=1)
            pos.append(jnp.where(found > 0.5, found - half, -9.0))
            mixes.append(jnp.concatenate(weight_parts[e], axis=1))
        return pos, mixes

    def pick_table(p, carry):
        pos, mixes = slot_tables(p)
        for g in range(CAP):
            hot = jnp.where(
                (pos[0] == 2.0 * g + 1.0) | (pos[1] == 2.0 * g - 6.0), 1.0, 0.0).astype(BF16)
            for q in range(lanes // 128):
                D[p, g * (lanes // 128) + q] = hot[:, q * 128:(q + 1) * 128]
        return carry

    lax.fori_loop(0, 3, pick_table, 0)

    def block_copy(p, c, step):
        spot, to = far_peer(p, step)
        return pltpu.make_async_remote_copy(
            O.at[c, :, spot], X.at[c, :, place(p)], d_send.at[c], d_recv.at[c],
            device_id=to, device_id_type=MESH)

    def own_block(p, c):
        return pltpu.make_async_copy(O.at[c, :, place(p)], X.at[c, :, place(p)], own_sem.at[c])

    def dispatch(r, carry):
        for q, p in enumerate(KINDS):
            c = r * 4 + q
            if p == 0:
                own_tokens(c).wait()
                for k in range(1, SIDE):
                    token_copy(c, k).wait_recv()
                tokens = T[c].reshape(lanes, n)
            else:
                own_tokens_other(p, r).wait()
                for k in range(1, SIDE):
                    token_copy_other(p, r, k).wait_recv()
                tokens = TO[p - 1, r].reshape(lanes, n)
            cut = lanes // 128
            picks = jnp.concatenate(
                [jnp.concatenate([D[p, g * cut + b] for b in range(cut)], axis=1)
                 for g in range(CAP)], axis=0)
            O[c] = jnp.dot(picks, tokens, preferred_element_type=F32).reshape(
                CAP, GROUP, 8, n).astype(BF16)
            for step in steps:
                block_copy(p, c, step).start()
            own_block(p, c).start()
        return carry

    lax.fori_loop(0, rounds, dispatch, 0)
    for r in range(rounds):
        for q, p in enumerate(KINDS):
            if p != 0:
                for k in range(1, SIDE):
                    token_copy(r * 4 + q, k).start()

    def sum_table(p, carry):
        pos, mixes = slot_tables(p)
        pos_t, mix_t = [v.T for v in pos], [v.T for v in mixes]
        for g in range(CAP):
            block = (jnp.where(pos_t[0] == 2.0 * g + 1.0, mix_t[0], 0.0)
                     + jnp.where(pos_t[1] == 2.0 * g - 6.0, mix_t[1], 0.0)).astype(BF16)
            for b in range(2):
                D[p, pl.ds((2 * g + b) * 2, 2)] = block[:, b * 128:(b + 1) * 128].reshape(
                    2, lanes // 2, 128)
        return carry

    lax.fori_loop(0, 3, sum_table, 0)
    acc[...] = jnp.zeros_like(acc)

    here = lax.broadcasted_iota(jnp.int32, (slots, slots), 0)
    there = lax.broadcasted_iota(jnp.int32, (slots, slots), 1)

    def reorder(p):
        scale = 16 if p == 1 else 64
        low, high = there % 4, (there // scale) % 4
        moved = there + (high - low) + (low - high) * scale
        return (here == moved).astype(F32).astype(BF16)

    def all_but_own(buf, sem):
        view = buf.at[:, pl.ds(0, GROUP - 1)]
        return pltpu.make_async_copy(view, view, sem)

    def up_step(r, carry):
        for b in range(2):
            m = 2 * r + b
            weight_copy(0, m).wait()
            weight_copy(1, m).wait()
            for q in (2 * b, 2 * b + 1):
                own_block(KINDS[q], r * 4 + q).wait()
                all_but_own(X.at[r * 4 + q], d_recv.at[r * 4 + q]).wait()
            p = KINDS[2 * b + 1]
            c = r * 4 + 2 * b
            straight = [X[c, g].reshape(slots, n) for g in range(CAP)]
            mixed = jnp.concatenate([X[c + 1, g].reshape(slots, n) for g in range(CAP)], axis=1)
            mixed = jnp.dot(reorder(p), mixed, preferred_element_type=F32).astype(BF16)
            both = [
                jnp.concatenate([straight[g], mixed[:, g * n:(g + 1) * n]], axis=1)
                for g in range(CAP)]
            for e in range(2):
                v = jnp.concatenate(both[3 * e:3 * e + 4], axis=0)
                acc[e, :, :ff] += jnp.dot(v, Wg[m, e], preferred_element_type=F32)
                acc[e, :, ff:] += jnp.dot(v, Wu[m, e], preferred_element_type=F32)
        return carry

    lax.fori_loop(0, rounds, up_step, 0)

    upper = (lax.broadcasted_iota(jnp.int32, (slots, ff), 0) % 8) // 4

    def hidden(g, carry):
        e, b = g // 4, g % 4
        part = pl.ds(pl.multiple_of(b * slots, slots), slots)
        h = silu_product(acc[e, part, :ff], acc[e, part, ff:])
        mixed_row = (g == 3).astype(jnp.int32) - (g == 4).astype(jnp.int32)
        keep = mixed_row * (2 * upper - 1) <= 0
        H[e, part, :] = jnp.where(keep, h, 0.0).astype(BF16)
        return carry

    lax.fori_loop(0, 8, hidden, 0)

    def back_copy(p, c, step):
        spot, to = far_peer(p, step)
        return pltpu.make_async_remote_copy(
            X.at[c, :, spot], Y.at[c, :, place(p)], y_send.at[c], y_recv.at[c],
            device_id=to, device_id_type=MESH)

    def own_back(p, c):
        return pltpu.make_async_copy(X.at[c, :, place(p)], Y.at[c, :, place(p)], yown_sem.at[c])

    def down_step(r, carry):
        for b in range(2):
            m = 2 * r + b
            weight_copy(2, m).wait()
            low = jnp.dot(H[0], Wd[m, 0], preferred_element_type=F32)
            high = jnp.dot(H[1], Wd[m, 1], preferred_element_type=F32)
            made = [low[g * slots:(g + 1) * slots] for g in range(3)]
            made.append(low[3 * slots:] + high[:slots])
            made += [high[g * slots:(g + 1) * slots] for g in range(1, 4)]
            c = r * 4 + 2 * b
            for g in range(CAP):
                X[c, g] = made[g][:, :n].reshape(GROUP, 8, n).astype(BF16)
            for step in steps:
                back_copy(0, c, step).start()
            own_back(0, c).start()
            p = KINDS[2 * b + 1]
            mixed = jnp.concatenate([v[:, n:].astype(BF16) for v in made], axis=1)
            mixed = jnp.dot(reorder(p), mixed, preferred_element_type=F32)
            for g in range(CAP):
                X[c + 1, g] = mixed[:, g * n:(g + 1) * n].reshape(GROUP, 8, n).astype(BF16)
            for step in steps:
                back_copy(p, c + 1, step).start()
            own_back(p, c + 1).start()
        return carry

    lax.fori_loop(0, rounds, down_step, 0)

    for which in range(3):
        small(which).wait()
    for r in range(rounds):
        for q, p in enumerate(KINDS):
            if p != 0:
                own_tokens(r * 4 + q).wait()
                for k in range(1, SIDE):
                    token_copy(r * 4 + q, k).wait_recv()
    shared[...] = jnp.zeros_like(shared)

    def shared_step(c, carry):
        tokens = T[c].reshape(lanes, n)
        span = pl.ds(pl.multiple_of(c * n, n), n)
        shared[0] += jnp.dot(tokens, Sg[0, span, :], preferred_element_type=F32)
        shared[1] += jnp.dot(tokens, Sg[1, span, :], preferred_element_type=F32)
        scored = tokens.astype(F32) * Gv[:, span].astype(F32)
        for q in range(n // 128):
            shared[2] += scored[:, q * 128:(q + 1) * 128]
        return carry

    lax.fori_loop(0, chunks, shared_step, 0)
    shared_hidden = silu_product(shared[0], shared[1]).astype(BF16)
    score = jnp.broadcast_to(jnp.sum(shared[2], axis=1, keepdims=True), (lanes, 128))
    shared[2] = 1.0 / (1.0 + jnp.exp(-score))

    def shared_part(c):
        span = pl.ds(pl.multiple_of(c * n, n), n)
        scale = jnp.concatenate([shared[2]] * (n // 128), axis=1)
        return scale * jnp.dot(shared_hidden, Sd[:, span], preferred_element_type=F32)

    def sum_copy(p, c, k):
        other, to = near(p, k)
        return pltpu.make_async_remote_copy(
            rs_out.at[c, other], rs_in.at[c, at[p]], r_send.at[c, k - 1], r_recv.at[c, k - 1],
            device_id=to, device_id_type=MESH)

    def shared_copy(m, k):
        other, to = near(0, k)
        return pltpu.make_async_remote_copy(
            sh_out.at[m, other], sh_in.at[m, x], s_send.at[m, k - 1], s_recv.at[m, k - 1],
            device_id=to, device_id_type=MESH)

    def shared_sums(m, carry):
        sh_out[m] = shared_part(2 * m + 1).reshape(SIDE, rows, n).astype(BF16)
        for k in range(1, SIDE):
            shared_copy(m, k).start()
        return carry

    lax.fori_loop(0, pairs, shared_sums, 0)

    def combine(r, carry):
        for q, p in enumerate(KINDS):
            c = r * 4 + q
            own_back(p, c).wait()
            all_but_own(Y.at[c], y_recv.at[c]).wait()
            table = jnp.concatenate(
                [D[p, 2 * b:2 * b + 2].reshape(lanes, 128) for b in range(2 * CAP)], axis=1)
            part = jnp.dot(
                table, Y[c].reshape(CAP * slots, n), preferred_element_type=F32)
            if p == 0:
                part = part + shared_part(c)
            own[...] = part.reshape(SIDE, rows, n)
            rs_out[c] = own[...].astype(BF16)
            for k in range(1, SIDE):
                sum_copy(p, c, k).start()
        return carry

    lax.fori_loop(0, rounds, combine, 0)

    def finish(r, carry):
        for q, p in enumerate(KINDS):
            c = r * 4 + q
            for k in range(1, SIDE):
                sum_copy(p, c, k).wait_recv()
            total = rs_out[c, at[p]].astype(F32)
            for k in range(1, SIDE):
                total = total + rs_in[c, near(p, k)[0]].astype(F32)
            if p != 0:
                m = c // 2
                for k in range(1, SIDE):
                    shared_copy(m, k).wait_recv()
                total = total + sh_out[m, x].astype(F32)
                for k in range(1, SIDE):
                    total = total + sh_in[m, near(0, k)[0]].astype(F32)
            out[:, pl.ds(pl.multiple_of(c * n, n), n)] = total.astype(BF16)
        return carry

    lax.fori_loop(0, rounds, finish, 0)

    for p in range(3):
        for k in range(1, SIDE):
            meta_copy(0, p, k).wait_send()
            meta_copy(1, p, k).wait_send()

    def drain(r, carry):
        for q, p in enumerate(KINDS):
            c = r * 4 + q
            for k in range(1, SIDE):
                token_copy(c, k).wait_send()
                sum_copy(p, c, k).wait_send()
                if p != 0:
                    token_copy_other(p, r, k).wait_send()
                    shared_copy(c // 2, k).wait_send()
            all_but_own(O.at[c], d_send.at[c]).wait()
            all_but_own(X.at[c], y_send.at[c]).wait()
        return carry

    lax.fori_loop(0, rounds, drain, 0)


def on_device(chunks, tokens, expert_ids, combine, w_gate, w_up, w_down, gate_up, down, gate_vec):
    rows, model = tokens.shape
    top = expert_ids.shape[1]
    ff, hid = w_gate.shape[2], down.shape[0]
    n = model // chunks
    slots = GROUP * 8
    lanes = SIDE * rows
    rounds, pairs = chunks // 4, chunks // 2
    near = SIDE - 1
    cfg = (chunks, n, rows, model, ff, hid, top)
    any_spec = pl.BlockSpec(memory_space=pl.ANY)
    dma = pltpu.SemaphoreType.DMA
    return pl.pallas_call(
        functools.partial(kernel, cfg),
        out_shape=jax.ShapeDtypeStruct((rows, model), BF16),
        in_specs=[any_spec] * 9,
        out_specs=pl.BlockSpec(memory_space=pltpu.VMEM),
        scratch_shapes=[
            pltpu.VMEM((chunks, SIDE, rows, n), BF16),
            pltpu.VMEM((2, rounds, SIDE, rows, n), BF16),
            pltpu.VMEM((3, SIDE, top, rows), jnp.int32),
            pltpu.VMEM((3, SIDE, top, rows), jnp.int32),
            pltpu.VMEM((3, 4 * CAP, 256, 128), BF16),
            pltpu.VMEM((chunks, CAP, GROUP, 8, n), BF16),
            pltpu.VMEM((chunks, CAP, GROUP, 8, n), BF16),
            pltpu.VMEM((chunks, CAP, GROUP, 8, n), BF16),
            pltpu.VMEM((pairs, 2, 2 * n, ff), BF16),
            pltpu.VMEM((pairs, 2, 2 * n, ff), BF16),
            pltpu.VMEM((pairs, 2, ff, 2 * n), BF16),
            pltpu.VMEM((2, 4 * slots, 2 * ff), F32),
            pltpu.VMEM((2, 4 * slots, ff), BF16),
            pltpu.VMEM((2, model, hid), BF16),
            pltpu.VMEM((hid, model), BF16),
            pltpu.VMEM((1, model), BF16),
            pltpu.VMEM((3, lanes, hid), F32),
            pltpu.VMEM((chunks, SIDE, rows, n), BF16),
            pltpu.VMEM((chunks, SIDE, rows, n), BF16),
            pltpu.VMEM((pairs, SIDE, rows, n), BF16),
            pltpu.VMEM((pairs, SIDE, rows, n), BF16),
            pltpu.VMEM((SIDE, rows, n), F32),
            dma((2, 3, near)), dma((2, 3, near)),
            dma((chunks, near)), dma((chunks, near)),
            dma((2, rounds, near)), dma((2, rounds, near)),
            dma((chunks,)), dma((chunks,)),
            dma((chunks,)), dma((chunks,)),
            dma((chunks, near)), dma((chunks, near)),
            dma((pairs, near)), dma((pairs, near)),
            dma((chunks,)), dma((2, rounds)), dma((3, pairs)),
            dma((chunks,)), dma((chunks,)), dma((9,)),
        ],
        compiler_params=pltpu.CompilerParams(
            collective_id=0, has_side_effects=True, vmem_limit_bytes=67043328),
    )(tokens, expert_ids.T, combine.T, w_gate, w_up, w_down, gate_up, down,
      gate_vec.reshape(1, model))


def solution(mesh, chunks=16):
    return jax.shard_map(
        functools.partial(on_device, chunks),
        mesh=mesh,
        in_specs=(
            P(("wide", "narrow"), None),
            P(("wide", "narrow"), None),
            P(("wide", "narrow"), None),
            P(("wide", "narrow"), None, None),
            P(("wide", "narrow"), None, None),
            P(("wide", "narrow"), None, None),
            P(None, None, "narrow"),
            P("narrow", None),
            P(),
        ),
        out_specs=P(("wide", "narrow"), None),
        check_vma=False,
    )
```

time: 391 us -> 161 us (0.41)
  waiting for transfers between devices: 176 us -> 0 us
  Pallas kernels: 0 us -> 157 us
  local copies, waits for them, and re-layouts: 135 us -> 3.17 us
  matrix products: 34.4 us -> 0 us
  starting transfers between devices: 27.2 us -> 0 us
  other arithmetic: 14.3 us -> 0 us
    all_to_all x4 -> x0, waiting for transfers between devices: 176 us -> none  [the longest x1 86.7 us: on_device(): lax.all_to_all(produced, ('wide', 'narrow'), split_axis=0, concat_axis=0,...]
    pallas_call x0 -> x1, Pallas kernels: none -> 157 us  [on_device(): pl.pallas_call(functools.partial(kernel, cfg), out_shape=jax.ShapeDtypeSt...]
    reshape x4 -> x1, local copies, waits for them, and re-layouts: 47.6 us -> 1.29 us  [on_device(): gate_vec.reshape(1, model)]
    dot_general x5 -> x0, matrix products: 34.4 us -> none  [the longest x1 18.6 us: expert_block(): jnp.einsum('secf,efd->secd', hidden, w_down, preferred_element_type=jnp.f...]
    all_to_all x4 -> x0, starting transfers between devices: 27.2 us -> none  [the longest x1 12 us: on_device(): lax.all_to_all(outgoing, ('wide', 'narrow'), split_axis=0, concat_axis=0,...]
    scatter x1 -> x0, local copies, waits for them, and re-layouts: 25.6 us -> none  [on_device(): jnp.zeros((experts_total * CAP, model_width), jnp.bfloat16).at[slot_index]]
    convert_element_type x2 -> x0, local copies, waits for them, and re-layouts: 25.2 us -> none  [the longest x1 14.7 us: expert_block(): jnp.einsum('secf,efd->secd', hidden, w_down, preferred_element_type=jnp.f...]
    gather x1 -> x0, local copies, waits for them, and re-layouts: 14.9 us -> none  [on_device(): returned[slot_index].reshape(tok_rows, top_count, model_width)]
  transfers between devices with their start and end apart: 4 -> 0, of which waited for: 3 -> 0; matrix products, arithmetic and copies ran while one was open for 32% -> 0% of each run, Pallas kernels for 0% -> 0%
where the time goes in v3:
time: 161 us; the launch traced here: 160 us
  Pallas kernels  157 us (98%)
  local copies, waits for them, and re-layouts  3.17 us (2%)
    pallas_call x1, Pallas kernels, on_device(): pl.pallas_call(functools.partial(kernel, cfg), out_shape=jax.ShapeDtypeSt...  157 us

profile of v3, /device:TPU:1, one launch (start us, length us, event | category | flops | bytes accessed | tf_op | source)
XLA Modules:
  0.0 160.0 jit_solution(4000561676272099320)
XLA Ops:
  0.0 1.3 reshape.3.gv
  1.3 156.8 %shard_map.91 = bf16[128,2048]{1,0:T(8,128)(2,1)} custom-call(bf16[128,2048]{1,0:T(8,128)(2,1)} %tok.1, s32[10,128]{1,0:T(8,128)} %bitcast.2, s32[10,128]{1,0:T(8,128)} %bitcast.3, bf16[2,2048,512]{2,1,0:T(8,128)(2,1)} %wg.1, bf16[2,2048,512]{2,1,0:T(8,128)(2,1)} %wu.1, bf16[2,512,2048]{2,1,0:T(8,128)(2,1)} %wd.1, bf16[2,2048,128]{2,1,0:T(8,128)(2,1)} %sgu.1, ...), custom_call_target="tpu_custom_call" | custom-call | tf_op jit(solution)/shard_map/pallas_call | solution.py:473
  158.1 1.9 %copy.11 = bf16[128,2048]{1,0:T(8,128)(2,1)} copy(bf16[128,2048]{1,0:T(8,128)(2,1)} %shard_map.91) | data formatting | bytes 1048576

commit v4 on v3

v4 whole, which is shorter than its diff:
```python
import functools

import jax
import jax.numpy as jnp
from jax import lax
from jax.experimental import pallas as pl
from jax.experimental.pallas import tpu as pltpu
from jax.sharding import PartitionSpec as P

CAP = 7
MESH = pl.DeviceIdType.MESH
F32 = jnp.float32
BF16 = jnp.bfloat16


SIDE = 4
GROUP = 2 * SIDE * SIDE
KINDS = (0, 1, 0, 2)
OUTWARD = ((0, 4), (4, 3))
HOMEWARD = ((0, 3), (3, 4))


def offsets():
    steps = [(da, db, dc) for da in range(SIDE) for db in range(SIDE) for dc in range(2)]
    steps = steps[1:]

    def far(step):
        return min(step[0], SIDE - step[0]) + min(step[1], SIDE - step[1])

    return sorted(steps, key=lambda s: (-far(s), (s[0] + 2 * s[1]) % 4, s[2]))


def silu_product(gate, up):
    return gate * (1.0 / (1.0 + jnp.exp(-gate))) * up


def kernel(
    cfg,
    tok, ids_in, mix_in, wg, wu, wd, sgu, sd, gv,
    out,
    T, TO, idv, mixv, D, O, X, Y, Wg, Wu, Wd, acc, H, Sg, Sd, Gv, shared, rs_in, sh_in,
    m_send, m_recv, t_send, t_recv, to_send, to_recv, d_send, d_recv, y_send, y_recv,
    r_send, r_recv, s_send, s_recv, loc, loco, w_sem, own_sem, yown_sem, small_sem,
):
    chunks, n, rows, model, ff, hid, top = cfg
    w = lax.axis_index("wide")
    x = lax.axis_index("narrow")
    core, y, z = w % 2, (w // 2) % SIDE, w // (2 * SIDE)
    at = (x, y, z)
    rounds, pairs = chunks // 4, chunks // 2
    lanes = SIDE * rows
    slots = GROUP * 8
    steps = offsets()

    def device(xx, yy, zz, cc):
        return ((zz * SIDE + yy) * 2 + cc, xx)

    def place(p):
        first, second = ((z, y), (z, x), (x, y))[p]
        return (first * SIDE + second) * 2 + core

    def far_peer(p, step):
        da, db, dc = step
        first, second = ((z, y), (z, x), (x, y))[p]
        first, second, cc = (first + da) % SIDE, (second + db) % SIDE, (core + dc) % 2
        spot = ((x, second, first), (second, y, first), (first, second, z))[p]
        return (first * SIDE + second) * 2 + cc, device(*spot, cc)

    def near(p, k):
        other = (at[p] + k) % SIDE
        spot = tuple(other if q == p else at[q] for q in range(3))
        return other, device(*spot, core)

    barrier = pltpu.get_barrier_semaphore()
    greeted = 0
    for dx in range(SIDE):
        for dy in range(SIDE):
            for dz in range(SIDE):
                for dc in range(2):
                    if dx * dy * dz == 0 and (dx, dy, dz, dc) != (0, 0, 0, 0):
                        greeted += 1
                        pl.semaphore_signal(
                            barrier, inc=1,
                            device_id=device((x + dx) % SIDE, (y + dy) % SIDE, (z + dz) % SIDE,
                                             (core + dc) % 2),
                            device_id_type=MESH)

    def weight_copy(which, m):
        cols = pl.ds(m * 2 * n, 2 * n)
        source = (wg.at[:, cols, :], wu.at[:, cols, :], wd.at[:, :, cols])[which]
        return pltpu.make_async_copy(source, (Wg, Wu, Wd)[which].at[m], w_sem.at[which, m])

    def own_tokens(c):
        return pltpu.make_async_copy(tok.at[:, pl.ds(c * n, n)], T.at[c, x], loc.at[c])

    def own_tokens_other(p, r):
        c = r * 4 + KINDS.index(p)
        return pltpu.make_async_copy(
            tok.at[:, pl.ds(c * n, n)], TO.at[p - 1, r, at[p]], loco.at[p - 1, r])

    def small(which):
        source = (sgu, sd, gv)[which]
        return pltpu.make_async_copy(source, (Sg, Sd, Gv)[which], small_sem.at[which])

    def own_meta(which, p):
        source, target = ((ids_in, idv), (mix_in, mixv))[which]
        return pltpu.make_async_copy(
            source, target.at[p, at[p]], small_sem.at[3 + which * 3 + p])

    for p in range(3):
        own_meta(0, p).start()
        own_meta(1, p).start()
    for c in range(chunks):
        own_tokens(c).start()
    for r in range(rounds):
        own_tokens_other(1, r).start()
        own_tokens_other(2, r).start()
    for which in range(3):
        small(which).start()

    pl.semaphore_wait(barrier, greeted)

    def meta_copy(which, p, k):
        source, target = ((ids_in, idv), (mix_in, mixv))[which]
        return pltpu.make_async_remote_copy(
            source, target.at[p, at[p]], m_send.at[which, p, k - 1], m_recv.at[which, p, k - 1],
            device_id=near(p, k)[1], device_id_type=MESH)

    def token_copy(c, k):
        return pltpu.make_async_remote_copy(
            tok.at[:, pl.ds(c * n, n)], T.at[c, x], t_send.at[c, k - 1], t_recv.at[c, k - 1],
            device_id=near(0, k)[1], device_id_type=MESH)

    def token_copy_other(p, r, k):
        c = r * 4 + KINDS.index(p)
        return pltpu.make_async_remote_copy(
            tok.at[:, pl.ds(c * n, n)], TO.at[p - 1, r, at[p]],
            to_send.at[p - 1, r, k - 1], to_recv.at[p - 1, r, k - 1],
            device_id=near(p, k)[1], device_id_type=MESH)

    for p in range(3):
        for k in range(1, SIDE):
            meta_copy(0, p, k).start()
            meta_copy(1, p, k).start()
    for r in range(rounds):
        for q, p in enumerate(KINDS):
            for k in range(1, SIDE):
                if p == 0:
                    token_copy(r * 4 + q, k).start()
                else:
                    token_copy_other(p, r, k).start()
    for m in range(pairs):
        for which in range(3):
            weight_copy(which, m).start()

    def meta_here(which, p):
        own_meta(which, p).wait()
        for k in range(1, SIDE):
            meta_copy(which, p, k).wait_recv()

    def table_for(p):
        meta_here(0, p)
        pick_table(p)

    pair = lax.broadcasted_iota(jnp.int32, (2 * GROUP, rows), 0)
    before = (
        lax.broadcasted_iota(jnp.int32, (rows, rows), 0)
        < lax.broadcasted_iota(jnp.int32, (rows, rows), 1)
    ).astype(F32).astype(BF16)
    rho = lax.broadcasted_iota(jnp.int32, (slots, 2 * GROUP), 0)
    col = lax.broadcasted_iota(jnp.int32, (slots, 2 * GROUP), 1)
    half = ((lax.broadcasted_iota(jnp.int32, (slots, lanes), 0) % 8) // 4).astype(F32)

    mine = (lax.broadcasted_iota(jnp.int32, (slots, lanes), 0) % 4) == (
        lax.broadcasted_iota(jnp.int32, (slots, lanes), 1) // rows)

    def slot_tables(p, weighted):
        by_first = jnp.where(p == 2, 2, 64)
        by_second = jnp.where(p == 1, 2, 16)
        base = jnp.where(p == 0, 2 * x, jnp.where(p == 1, 16 * y, 64 * z))
        expert = (
            base + (pair // 16) * by_first + ((pair // 4) % 4) * by_second
            + ((pair // 2) % 2) * 8 + pair % 2)
        spots, weights = [], []
        for s in range(SIDE):
            chosen = jnp.zeros((2 * GROUP, rows), F32)
            weight = jnp.zeros((2 * GROUP, rows), F32)
            for k in range(top):
                hit = jnp.broadcast_to(idv[p, s, k:k + 1, :], (2 * GROUP, rows)) == expert
                chosen = jnp.where(hit, 1.0, chosen)
                if weighted:
                    mix = mixv[p, s, k:k + 1, :].astype(F32) * (1.0 / 256.0)
                    weight = jnp.where(hit, jnp.broadcast_to(mix, (2 * GROUP, rows)), weight)
            rank = jnp.dot(chosen.astype(BF16), before, preferred_element_type=F32)
            spots.append(jnp.where(chosen > 0.5, rank + 1.0, 0.0).astype(BF16))
            weights.append(weight.astype(BF16))
        spot = jnp.concatenate(spots, axis=1)
        weight = jnp.concatenate(weights, axis=1)
        pos, mixes = [], []
        for e in range(2):
            spread = (col == (rho // 8) * 2 + e).astype(F32).astype(BF16)
            found = jnp.dot(spread, spot, preferred_element_type=F32)
            pos.append(jnp.where(mine & (found > 0.5), found - half, -9.0))
            if weighted:
                mixes.append(jnp.dot(spread, weight, preferred_element_type=F32))
        return pos, mixes

    def pick_table(p):
        pos, _ = slot_tables(p, False)
        for g in range(CAP):
            hot = jnp.where(
                (pos[0] == 2.0 * g + 1.0) | (pos[1] == 2.0 * g - 6.0), 1.0, 0.0).astype(BF16)
            for q in range(lanes // 128):
                D[p, g * (lanes // 128) + q] = hot[:, q * 128:(q + 1) * 128]

    def block_copy(p, c, step, h):
        spot, to = far_peer(p, step)
        span = pl.ds(*OUTWARD[h])
        return pltpu.make_async_remote_copy(
            O.at[c, span, spot], X.at[c, span, place(p)], d_send.at[h, c], d_recv.at[h, c],
            device_id=to, device_id_type=MESH)

    def own_block(p, c, h):
        span = pl.ds(*OUTWARD[h])
        return pltpu.make_async_copy(
            O.at[c, span, place(p)], X.at[c, span, place(p)], own_sem.at[h, c])

    def send_blocks(p, c, h):
        for step in steps:
            block_copy(p, c, step, h).start()
        own_block(p, c, h).start()

    def send_rows(r, q):
        p, c = KINDS[q], r * 4 + q
        if p == 0:
            own_tokens(c).wait()
            for k in range(1, SIDE):
                token_copy(c, k).wait_recv()
            tokens = T[c].reshape(lanes, n)
        else:
            own_tokens_other(p, r).wait()
            for k in range(1, SIDE):
                token_copy_other(p, r, k).wait_recv()
            tokens = TO[p - 1, r].reshape(lanes, n)
        cut = lanes // 128
        picks = jnp.concatenate(
            [jnp.concatenate([D[p, g * cut + b] for b in range(cut)], axis=1)
             for g in range(CAP)], axis=0)
        O[c] = jnp.dot(picks, tokens, preferred_element_type=F32).reshape(
            CAP, GROUP, 8, n).astype(BF16)
        send_blocks(p, c, 0)

    def dispatch(r, carry):
        for q in range(4):
            send_rows(r, q)
        return carry

    for q in (0, 1, 3, 2):
        if q < 2 or q == 3:
            table_for(KINDS[q])
        send_rows(0, q)
    lax.fori_loop(1, rounds, dispatch, 0)

    def second_half(r, carry):
        for q, p in enumerate(KINDS):
            send_blocks(p, r * 4 + q, 1)
        return carry

    lax.fori_loop(0, rounds, second_half, 0)
    for r in range(rounds):
        for q, p in enumerate(KINDS):
            if p != 0:
                for k in range(1, SIDE):
                    token_copy(r * 4 + q, k).start()

    for p in range(3):
        meta_here(1, p)

    def sum_table(p, carry):
        pos, mixes = slot_tables(p, True)
        pos_t, mix_t = [v.T for v in pos], [v.T for v in mixes]
        for g in range(CAP):
            block = (jnp.where(pos_t[0] == 2.0 * g + 1.0, mix_t[0], 0.0)
                     + jnp.where(pos_t[1] == 2.0 * g - 6.0, mix_t[1], 0.0)).astype(BF16)
            for b in range(2):
                D[p, pl.ds((2 * g + b) * 2, 2)] = block[:, b * 128:(b + 1) * 128].reshape(
                    2, lanes // 2, 128)
        return carry

    lax.fori_loop(0, 3, sum_table, 0)

    here = lax.broadcasted_iota(jnp.int32, (slots, slots), 0)
    there = lax.broadcasted_iota(jnp.int32, (slots, slots), 1)

    def reorder(p):
        scale = 16 if p == 1 else 64
        low, high = there % 4, (there // scale) % 4
        moved = there + (high - low) + (low - high) * scale
        return (here == moved).astype(F32).astype(BF16)

    def all_but_own(buf, part, sem):
        view = buf.at[pl.ds(*part), pl.ds(0, GROUP - 1)]
        return pltpu.make_async_copy(view, view, sem)

    def back_copy(p, c, step, h):
        spot, to = far_peer(p, step)
        span = pl.ds(*HOMEWARD[h])
        return pltpu.make_async_remote_copy(
            X.at[c, span, spot], Y.at[c, span, place(p)], y_send.at[h, c], y_recv.at[h, c],
            device_id=to, device_id_type=MESH)

    def own_back(p, c, h):
        span = pl.ds(*HOMEWARD[h])
        return pltpu.make_async_copy(
            X.at[c, span, place(p)], Y.at[c, span, place(p)], yown_sem.at[h, c])

    def send_back(p, c, h):
        for step in steps:
            back_copy(p, c, step, h).start()
        own_back(p, c, h).start()

    upper = (lax.broadcasted_iota(jnp.int32, (slots, ff), 0) % 8) // 4

    for e in range(2):
        acc[...] = jnp.zeros_like(acc)

        def up_step(r, carry):
            for b in range(2):
                m = 2 * r + b
                if e == 0:
                    weight_copy(0, m).wait()
                    weight_copy(1, m).wait()
                for q in (2 * b, 2 * b + 1):
                    own_block(KINDS[q], r * 4 + q, e).wait()
                    all_but_own(X.at[r * 4 + q], OUTWARD[e], d_recv.at[e, r * 4 + q]).wait()
                p = KINDS[2 * b + 1]
                c = r * 4 + 2 * b
                mixed = jnp.concatenate(
                    [X[c + 1, 3 * e + g].reshape(slots, n) for g in range(4)], axis=1)
                mixed = jnp.dot(reorder(p), mixed, preferred_element_type=F32).astype(BF16)
                v = jnp.concatenate(
                    [jnp.concatenate(
                        [X[c, 3 * e + g].reshape(slots, n), mixed[:, g * n:(g + 1) * n]], axis=1)
                     for g in range(4)], axis=0)
                acc[:, :ff] += jnp.dot(v, Wg[m, e], preferred_element_type=F32)
                acc[:, ff:] += jnp.dot(v, Wu[m, e], preferred_element_type=F32)
            return carry

        lax.fori_loop(0, rounds, up_step, 0)

        def hidden(g, carry):
            part = pl.ds(pl.multiple_of(g * slots, slots), slots)
            h = silu_product(acc[part, :ff], acc[part, ff:])
            mixed_row = (g == 3 * (1 - e)).astype(jnp.int32)
            keep = mixed_row * (upper - e) * (1 - 2 * e) <= 0
            H[e, part, :] = jnp.where(keep, h, 0.0).astype(BF16)
            return carry

        lax.fori_loop(0, 4, hidden, 0)

        def down_step(r, carry):
            for b in range(2):
                m = 2 * r + b
                c = r * 4 + 2 * b
                if e == 0:
                    weight_copy(2, m).wait()
                    low = jnp.dot(H[0, :3 * slots], Wd[m, 0], preferred_element_type=F32)
                    made = [low[g * slots:(g + 1) * slots] for g in range(3)]
                else:
                    high = jnp.dot(H[1], Wd[m, 1], preferred_element_type=F32)
                    low = jnp.dot(H[0, 3 * slots:], Wd[m, 0], preferred_element_type=F32)
                    made = [low + high[:slots]]
                    made += [high[g * slots:(g + 1) * slots] for g in range(1, 4)]
                first = HOMEWARD[e][0]
                for g, v in enumerate(made):
                    X[c, first + g] = v[:, :n].reshape(GROUP, 8, n).astype(BF16)
                send_back(0, c, e)
                p = KINDS[2 * b + 1]
                mixed = jnp.concatenate([v[:, n:].astype(BF16) for v in made], axis=1)
                mixed = jnp.dot(reorder(p), mixed, preferred_element_type=F32)
                for g in range(len(made)):
                    X[c + 1, first + g] = mixed[:, g * n:(g + 1) * n].reshape(
                        GROUP, 8, n).astype(BF16)
                send_back(p, c + 1, e)
            return carry

        lax.fori_loop(0, rounds, down_step, 0)

    for which in range(3):
        small(which).wait()
    for r in range(rounds):
        for q, p in enumerate(KINDS):
            if p != 0:
                own_tokens(r * 4 + q).wait()
                for k in range(1, SIDE):
                    token_copy(r * 4 + q, k).wait_recv()
    shared[...] = jnp.zeros_like(shared)

    def shared_step(c, carry):
        tokens = T[c].reshape(lanes, n)
        span = pl.ds(pl.multiple_of(c * n, n), n)
        shared[0] += jnp.dot(tokens, Sg[0, span, :], preferred_element_type=F32)
        shared[1] += jnp.dot(tokens, Sg[1, span, :], preferred_element_type=F32)
        scored = tokens.astype(F32) * Gv[:, span].astype(F32)
        for q in range(n // 128):
            shared[2] += scored[:, q * 128:(q + 1) * 128]
        return carry

    lax.fori_loop(0, chunks, shared_step, 0)
    shared_hidden = silu_product(shared[0], shared[1]).astype(BF16)
    score = jnp.broadcast_to(jnp.sum(shared[2], axis=1, keepdims=True), (lanes, 128))
    shared[2] = 1.0 / (1.0 + jnp.exp(-score))

    def shared_part(c):
        span = pl.ds(pl.multiple_of(c * n, n), n)
        scale = jnp.concatenate([shared[2]] * (n // 128), axis=1)
        return scale * jnp.dot(shared_hidden, Sd[:, span], preferred_element_type=F32)

    tall = rows // 8

    def spot_of(c, which, s):
        return O.at[c, 2 * which + s // 2, pl.ds(pl.multiple_of((s % 2) * tall, tall), tall)]

    def taken(ref):
        return ref[...].astype(F32).reshape(rows, n)

    def sum_copy(p, c, k):
        other, to = near(p, k)
        return pltpu.make_async_remote_copy(
            spot_of(c, 0, other), rs_in.at[c, at[p]], r_send.at[c, k - 1], r_recv.at[c, k - 1],
            device_id=to, device_id_type=MESH)

    def shared_copy(m, k):
        other, to = near(0, k)
        return pltpu.make_async_remote_copy(
            spot_of(2 * m + 1, 1, other), sh_in.at[m, x], s_send.at[m, k - 1], s_recv.at[m, k - 1],
            device_id=to, device_id_type=MESH)

    def sent(c, carry):
        for h in range(2):
            all_but_own(O.at[c], OUTWARD[h], d_send.at[h, c]).wait()
        return carry

    lax.fori_loop(0, chunks, sent, 0)

    def shared_sums(m, carry):
        O[2 * m + 1, 2:4] = shared_part(2 * m + 1).reshape(2, GROUP, 8, n).astype(BF16)
        for k in range(1, SIDE):
            shared_copy(m, k).start()
        return carry

    lax.fori_loop(0, pairs, shared_sums, 0)

    def finish(r, carry):
        for q, p in enumerate(KINDS):
            c = r * 4 + q
            for k in range(1, SIDE):
                sum_copy(p, c, k).wait_recv()
            total = taken(spot_of(c, 0, at[p]))
            for k in range(1, SIDE):
                total = total + taken(rs_in.at[c, near(p, k)[0]])
            if p != 0:
                m = c // 2
                for k in range(1, SIDE):
                    shared_copy(m, k).wait_recv()
                total = total + taken(spot_of(c, 1, x))
                for k in range(1, SIDE):
                    total = total + taken(sh_in.at[m, near(0, k)[0]])
            out[:, pl.ds(pl.multiple_of(c * n, n), n)] = total.astype(BF16)
        return carry

    def combine(r, carry):
        for q, p in enumerate(KINDS):
            c = r * 4 + q
            for h in range(2):
                own_back(p, c, h).wait()
                all_but_own(Y.at[c], HOMEWARD[h], y_recv.at[h, c]).wait()
            table = jnp.concatenate(
                [D[p, 2 * b:2 * b + 2].reshape(lanes, 128) for b in range(2 * CAP)], axis=1)
            part = jnp.dot(
                table, Y[c].reshape(CAP * slots, n), preferred_element_type=F32)
            if p == 0:
                part = part + shared_part(c)
            O[c, 0:2] = part.reshape(2, GROUP, 8, n).astype(BF16)
            for k in range(1, SIDE):
                sum_copy(p, c, k).start()
        return carry

    lax.fori_loop(0, rounds, combine, 0)

    lax.fori_loop(0, rounds, finish, 0)

    for p in range(3):
        for k in range(1, SIDE):
            meta_copy(0, p, k).wait_send()
            meta_copy(1, p, k).wait_send()

    def drain(r, carry):
        for q, p in enumerate(KINDS):
            c = r * 4 + q
            for k in range(1, SIDE):
                token_copy(c, k).wait_send()
                sum_copy(p, c, k).wait_send()
                if p != 0:
                    token_copy_other(p, r, k).wait_send()
                    shared_copy(c // 2, k).wait_send()
            for h in range(2):
                all_but_own(X.at[c], HOMEWARD[h], y_send.at[h, c]).wait()
        return carry

    lax.fori_loop(0, rounds, drain, 0)


def on_device(chunks, tokens, expert_ids, combine, w_gate, w_up, w_down, gate_up, down, gate_vec):
    rows, model = tokens.shape
    top = expert_ids.shape[1]
    ff, hid = w_gate.shape[2], down.shape[0]
    n = model // chunks
    slots = GROUP * 8
    lanes = SIDE * rows
    rounds, pairs = chunks // 4, chunks // 2
    near = SIDE - 1
    cfg = (chunks, n, rows, model, ff, hid, top)
    any_spec = pl.BlockSpec(memory_space=pl.ANY)
    dma = pltpu.SemaphoreType.DMA
    return pl.pallas_call(
        functools.partial(kernel, cfg),
        out_shape=jax.ShapeDtypeStruct((rows, model), BF16),
        in_specs=[any_spec] * 9,
        out_specs=pl.BlockSpec(memory_space=pltpu.VMEM),
        scratch_shapes=[
            pltpu.VMEM((chunks, SIDE, rows, n), BF16),
            pltpu.VMEM((2, rounds, SIDE, rows, n), BF16),
            pltpu.VMEM((3, SIDE, top, rows), jnp.int32),
            pltpu.VMEM((3, SIDE, top, rows), jnp.int32),
            pltpu.VMEM((3, 4 * CAP, 256, 128), BF16),
            pltpu.VMEM((chunks, CAP, GROUP, 8, n), BF16),
            pltpu.VMEM((chunks, CAP, GROUP, 8, n), BF16),
            pltpu.VMEM((chunks, CAP, GROUP, 8, n), BF16),
            pltpu.VMEM((pairs, 2, 2 * n, ff), BF16),
            pltpu.VMEM((pairs, 2, 2 * n, ff), BF16),
            pltpu.VMEM((pairs, 2, ff, 2 * n), BF16),
            pltpu.VMEM((4 * slots, 2 * ff), F32),
            pltpu.VMEM((2, 4 * slots, ff), BF16),
            pltpu.VMEM((2, model, hid), BF16),
            pltpu.VMEM((hid, model), BF16),
            pltpu.VMEM((1, model), BF16),
            pltpu.VMEM((3, lanes, hid), F32),
            pltpu.VMEM((chunks, SIDE, rows // 8, 8, n), BF16),
            pltpu.VMEM((pairs, SIDE, rows // 8, 8, n), BF16),
            dma((2, 3, near)), dma((2, 3, near)),
            dma((chunks, near)), dma((chunks, near)),
            dma((2, rounds, near)), dma((2, rounds, near)),
            dma((2, chunks)), dma((2, chunks)),
            dma((2, chunks)), dma((2, chunks)),
            dma((chunks, near)), dma((chunks, near)),
            dma((pairs, near)), dma((pairs, near)),
            dma((chunks,)), dma((2, rounds)), dma((3, pairs)),
            dma((2, chunks)), dma((2, chunks)), dma((9,)),
        ],
        compiler_params=pltpu.CompilerParams(
            collective_id=0, has_side_effects=True, vmem_limit_bytes=67043328),
    )(tokens, expert_ids.T, combine.T, w_gate, w_up, w_down, gate_up, down,
      gate_vec.reshape(1, model))


def solution(mesh, chunks=8):
    return jax.shard_map(
        functools.partial(on_device, chunks),
        mesh=mesh,
        in_specs=(
            P(("wide", "narrow"), None),
            P(("wide", "narrow"), None),
            P(("wide", "narrow"), None),
            P(("wide", "narrow"), None, None),
            P(("wide", "narrow"), None, None),
            P(("wide", "narrow"), None, None),
            P(None, None, "narrow"),
            P("narrow", None),
            P(),
        ),
        out_specs=P(("wide", "narrow"), None),
        check_vma=False,
    )
```

time: 161 us -> 154 us (0.957)
  Pallas kernels: 157 us -> 151 us
    pallas_call x1, Pallas kernels: 157 us -> 151 us  [on_device(): pl.pallas_call(functools.partial(kernel, cfg), out_shape=jax.ShapeDtypeSt...]
where the time goes in v4:
time: 154 us
  Pallas kernels  151 us (98%)
  local copies, waits for them, and re-layouts  3.17 us (2%)
    pallas_call x1, Pallas kernels, on_device(): pl.pallas_call(functools.partial(kernel, cfg), out_shape=jax.ShapeDtypeSt...  151 us

profile of v4, /device:TPU:1, one launch (start us, length us, event | category | flops | bytes accessed | tf_op | source)
XLA Modules:
  0.0 154.0 jit_solution(13512010449748967638)
XLA Ops:
  0.0 1.3 reshape.3.gv
  1.3 150.8 %shard_map.91 = bf16[128,2048]{1,0:T(8,128)(2,1)} custom-call(bf16[128,2048]{1,0:T(8,128)(2,1)} %tok.1, s32[10,128]{1,0:T(8,128)} %bitcast.2, s32[10,128]{1,0:T(8,128)} %bitcast.3, bf16[2,2048,512]{2,1,0:T(8,128)(2,1)} %wg.1, bf16[2,2048,512]{2,1,0:T(8,128)(2,1)} %wu.1, bf16[2,512,2048]{2,1,0:T(8,128)(2,1)} %wd.1, bf16[2,2048,128]{2,1,0:T(8,128)(2,1)} %sgu.1, ...), custom_call_target="tpu_custom_call" | custom-call | tf_op jit(solution)/shard_map/pallas_call | solution.py:526
  152.1 1.9 %copy.11 = bf16[128,2048]{1,0:T(8,128)(2,1)} copy(bf16[128,2048]{1,0:T(8,128)(2,1)} %shard_map.91) | data formatting | bytes 1048576

commit v5 on v4

--- a/solution.py
+++ b/solution.py
@@ -27,7 +27,13 @@
     def far(step):
         return min(step[0], SIDE - step[0]) + min(step[1], SIDE - step[1])
 
-    return sorted(steps, key=lambda s: (-far(s), (s[0] + 2 * s[1]) % 4, s[2]))
+    ordered = sorted(steps, key=lambda s: (-far(s), (s[0] + 2 * s[1]) % 4, s[2]))
+    mixed = []
+    while ordered:
+        mixed.append(ordered.pop(0))
+        if ordered:
+            mixed.append(ordered.pop())
+    return mixed
 
 
 def silu_product(gate, up):

time: 154 us -> 152 us (0.987)
  Pallas kernels: 151 us -> 149 us
    pallas_call x1, Pallas kernels: 151 us -> 149 us  [on_device(): pl.pallas_call(functools.partial(kernel, cfg), out_shape=jax.ShapeDtypeSt...]
where the time goes in v5:
time: 152 us
  Pallas kernels  149 us (98%)
  local copies, waits for them, and re-layouts  3.17 us (2%)
    pallas_call x1, Pallas kernels, on_device(): pl.pallas_call(functools.partial(kernel, cfg), out_shape=jax.ShapeDtypeSt...  149 us

profile of v5, /device:TPU:1, one launch (start us, length us, event | category | flops | bytes accessed | tf_op | source)
XLA Modules:
  0.0 151.7 jit_solution(10325432812307052978)
XLA Ops:
  0.0 1.3 reshape.3.gv
  1.3 148.5 %shard_map.91 = bf16[128,2048]{1,0:T(8,128)(2,1)} custom-call(bf16[128,2048]{1,0:T(8,128)(2,1)} %tok.1, s32[10,128]{1,0:T(8,128)} %bitcast.2, s32[10,128]{1,0:T(8,128)} %bitcast.3, bf16[2,2048,512]{2,1,0:T(8,128)(2,1)} %wg.1, bf16[2,2048,512]{2,1,0:T(8,128)(2,1)} %wu.1, bf16[2,512,2048]{2,1,0:T(8,128)(2,1)} %wd.1, bf16[2,2048,128]{2,1,0:T(8,128)(2,1)} %sgu.1, ...), custom_call_target="tpu_custom_call" | custom-call | tf_op jit(solution)/shard_map/pallas_call | solution.py:532
  149.8 1.9 %copy.11 = bf16[128,2048]{1,0:T(8,128)(2,1)} copy(bf16[128,2048]{1,0:T(8,128)(2,1)} %shard_map.91) | data formatting | bytes 1048576

commit v6 on v5

--- a/solution.py
+++ b/solution.py
@@ -407,7 +407,7 @@
         span = pl.ds(pl.multiple_of(c * n, n), n)
         shared[0] += jnp.dot(tokens, Sg[0, span, :], preferred_element_type=F32)
         shared[1] += jnp.dot(tokens, Sg[1, span, :], preferred_element_type=F32)
-        scored = tokens.astype(F32) * Gv[:, span].astype(F32)
+        scored = tokens.astype(F32) * Gv[span].reshape(1, n).astype(F32)
         for q in range(n // 128):
             shared[2] += scored[:, q * 128:(q + 1) * 128]
         return carry
@@ -550,7 +550,7 @@
             pltpu.VMEM((2, 4 * slots, ff), BF16),
             pltpu.VMEM((2, model, hid), BF16),
             pltpu.VMEM((hid, model), BF16),
-            pltpu.VMEM((1, model), BF16),
+            pltpu.VMEM((model,), BF16),
             pltpu.VMEM((3, lanes, hid), F32),
             pltpu.VMEM((chunks, SIDE, rows // 8, 8, n), BF16),
             pltpu.VMEM((pairs, SIDE, rows // 8, 8, n), BF16),
@@ -567,7 +567,7 @@
         compiler_params=pltpu.CompilerParams(
             collective_id=0, has_side_effects=True, vmem_limit_bytes=67043328),
     )(tokens, expert_ids.T, combine.T, w_gate, w_up, w_down, gate_up, down,
-      gate_vec.reshape(1, model))
+      gate_vec)
 
 
 def solution(mesh, chunks=8):

time: 152 us -> 151 us (level)
  no operation moved by 1% of the time
where the time goes in v6:
time: 151 us; the launch traced here: 150 us
  Pallas kernels  149 us (99%)
  local copies, waits for them, and re-layouts  1.88 us (1%)
    pallas_call x1, Pallas kernels, on_device(): pl.pallas_call(functools.partial(kernel, cfg), out_shape=jax.ShapeDtypeSt...  149 us

profile of v6, /device:TPU:1, one launch (start us, length us, event | category | flops | bytes accessed | tf_op | source)
XLA Modules:
  0.0 150.5 jit_solution(18230104670065897492)
XLA Ops:
  0.0 148.6 %shard_map.91 = bf16[128,2048]{1,0:T(8,128)(2,1)} custom-call(bf16[128,2048]{1,0:T(8,128)(2,1)} %tok.1, s32[10,128]{1,0:T(8,128)} %bitcast.2, s32[10,128]{1,0:T(8,128)} %bitcast.3, bf16[2,2048,512]{2,1,0:T(8,128)(2,1)} %wg.1, bf16[2,2048,512]{2,1,0:T(8,128)(2,1)} %wu.1, bf16[2,512,2048]{2,1,0:T(8,128)(2,1)} %wd.1, bf16[2,2048,128]{2,1,0:T(8,128)(2,1)} %sgu.1, ...), custom_call_target="tpu_custom_call" | custom-call | tf_op jit(solution)/shard_map/pallas_call | solution.py:532
  148.6 1.9 %copy.11 = bf16[128,2048]{1,0:T(8,128)(2,1)} copy(bf16[128,2048]{1,0:T(8,128)(2,1)} %shard_map.91) | data formatting | bytes 1048576
